TPU v7x, 32 devices: a whole 2x2x4 slice. The times are simulated.
32 devices in a mesh: ctx: 8 (over y, x, core), tp: 4 (over z).
Axes of the slice: x: 2, y: 2, z: 4, core: 2. Of those that a mesh axis runs over, the one named last changes fastest.
Arguments:
- query_proj: bfloat16 [8192, 8192], P('ctx', 'tp'), may hold values from -6 to 6
- key_proj: bfloat16 [8192, 8192], P('ctx', 'tp'), may hold values from -6 to 6
- value_proj: bfloat16 [8192, 8192], P('ctx', 'tp'), may hold values from -6 to 6
- cotangent: bfloat16 [8192, 8192], P('ctx', 'tp'), may hold values from -6 to 6
- short_taps: float32 [3, 3, 8192], P(None, None, 'tp'), may hold values from -2.5 to 2.5
- residues: float32 [512, 16], P('tp'), may hold values from -0.6 to 0.6
- decay_rates: float32 [512, 16], P('tp'), may hold values from 3.6621095e-05 to 0.08
Outputs:
- mixed: bfloat16 [8192, 8192], P('ctx', 'tp')
- grad_query: bfloat16 [8192, 8192], P('ctx', 'tp')
- grad_key: bfloat16 [8192, 8192], P('ctx', 'tp')
- grad_value: bfloat16 [8192, 8192], P('ctx', 'tp')
- grad_taps: float32 [3, 3, 8192], P(None, None, 'tp')
- grad_residues: float32 [512, 16], P('tp')
All inputs are finite; a program needn't handle non-finite values.
Results may differ from a plain program's by a relative error of at most 0.014.
Values may be sent and summed in bfloat16 or wider, within the bound.
No kernel may reach another device: no remote copies, remote signals or barrier semaphores. Data moves between devices by JAX's collectives and lax.ppermute only.
A program may use at most 128 MiB of HBM per device.

v0:
```python
import jax
import jax.numpy as jnp
from jax import lax
from jax.sharding import PartitionSpec as P


def from_behind(value, axis, steps):
    count = lax.axis_size(axis)
    initial, last = (max(0, -steps), min(count, count - steps))
    return lax.ppermute(value, axis, [(source, source + steps) for source in range(initial, last)])


def kernel_tables(residues, decay_rates, block_len):
    offsets = jnp.arange(block_len, dtype=jnp.float32)
    spread = offsets[:, None] - offsets[None, :]
    causal = spread >= 0.0
    lagged = jnp.maximum(spread, 0.0)
    toeplitz = jnp.zeros((residues.shape[0], block_len, block_len), jnp.float32)
    for mode_index in range(residues.shape[1]):
        rate = decay_rates[:, mode_index][:, None, None]
        toeplitz = toeplitz + residues[:, mode_index][:, None, None] * jnp.exp(-rate * lagged[None])
    toeplitz = jnp.where(causal[None], toeplitz, jnp.zeros_like(toeplitz))
    readin = residues[:, :, None] * jnp.exp(
        -decay_rates[:, :, None] * (offsets + 1.0)[None, None, :]
    )
    absorb = jnp.exp(-decay_rates[:, :, None] * (block_len - 1.0 - offsets)[None, None, :])
    passing = jnp.exp(-decay_rates * block_len)
    return (toeplitz, readin, absorb, passing)


def chain_combine(earlier, later):
    return (earlier[0] * later[0], later[1] + later[0] * earlier[1])


def modal_conv(columns, residues, decay_rates):
    width, length = columns.shape
    groups, modes = residues.shape
    members = width // groups
    block_len = min(128, length)
    count = length // block_len
    toeplitz, readin, absorb, passing = kernel_tables(residues, decay_rates, block_len)
    blocks = columns.reshape(groups, members, count, block_len)
    inner = jnp.einsum("gts,gkns->gknt", toeplitz, blocks, precision=lax.Precision.HIGHEST)
    ends = jnp.einsum("gms,gkns->nmgk", absorb, blocks, precision=lax.Precision.HIGHEST).reshape(
        count, modes, width
    )
    rate_columns = jnp.repeat(passing.T, members, axis=1)
    factors = jnp.broadcast_to(rate_columns[None], (count, modes, width))
    after_block = lax.associative_scan(chain_combine, (factors, ends), axis=0)[1]
    before = jnp.concatenate([jnp.zeros((1, modes, width), jnp.float32), after_block[:-1]], axis=0)
    carried = jnp.einsum(
        "gmt,nmgk->gknt",
        readin,
        before.reshape(count, modes, groups, members),
        precision=lax.Precision.HIGHEST,
    )
    return ((inner + carried).reshape(width, length), after_block[-1])


def short_forward(stream, prior, taps):
    span = taps.shape[0] - 1
    length = stream.shape[0]
    extended = jnp.concatenate([prior, stream], axis=0)
    total = jnp.zeros(stream.shape, jnp.float32)
    for lag_index in range(taps.shape[0]):
        window = extended[span - lag_index : span - lag_index + length].astype(jnp.float32)
        total = total + taps[lag_index][None, :] * window
    return total


def short_backward(grad_out, after, stream, prior, taps):
    span = taps.shape[0] - 1
    length = stream.shape[0]
    extended = jnp.concatenate([prior, stream], axis=0)
    extended_grad = jnp.concatenate([grad_out, after], axis=0)
    grad_in = jnp.zeros(grad_out.shape, jnp.float32)
    tap_rows = []
    for lag_index in range(taps.shape[0]):
        grad_in = grad_in + taps[lag_index][None, :] * extended_grad[lag_index : lag_index + length]
        window = extended[span - lag_index : span - lag_index + length].astype(jnp.float32)
        tap_rows.append(jnp.sum(grad_out * window, axis=0))
    return (grad_in, jnp.stack(tap_rows))


def local(query_proj, key_proj, value_proj, cotangent, short_taps, residues, decay_rates):
    length, width = query_proj.shape
    span = short_taps.shape[1] - 1
    priors = from_behind(
        (query_proj[length - span :], key_proj[length - span :], value_proj[length - span :]),
        "ctx",
        1,
    )
    query_short = short_forward(query_proj, priors[0], short_taps[0])
    key_short = short_forward(key_proj, priors[1], short_taps[1])
    value_short = short_forward(value_proj, priors[2], short_taps[2])
    gated_low = (key_short * value_short).astype(jnp.bfloat16)
    gated_cols_low = gated_low.T
    slab_groups = residues.shape[0] // lax.axis_size("ctx")
    first_group = lax.axis_index("ctx") * slab_groups
    slab_residues = lax.dynamic_slice_in_dim(residues, first_group, slab_groups, 0)
    slab_rates = lax.dynamic_slice_in_dim(decay_rates, first_group, slab_groups, 0)
    columns = lax.all_to_all(gated_cols_low, "ctx", split_axis=0, concat_axis=1, tiled=True)
    outputs, unwind = jax.vjp(
        lambda signal, weights: modal_conv(signal, weights, slab_rates),
        columns.astype(jnp.float32),
        slab_residues,
    )
    slab_out, slab_final = outputs
    long_cols_low = lax.all_to_all(
        slab_out.astype(jnp.bfloat16), "ctx", split_axis=1, concat_axis=0, tiled=True
    )
    long_low = long_cols_low.T
    long_out = lax.optimization_barrier(long_low).astype(jnp.float32)
    mixed = (query_short * long_out).astype(jnp.bfloat16)
    grad_cot = cotangent.astype(jnp.float32)
    grad_qshort = grad_cot * long_out
    grad_long_low = (grad_cot * query_short).astype(jnp.bfloat16)
    grad_cols_low = grad_long_low.T
    grad_columns = lax.all_to_all(grad_cols_low, "ctx", split_axis=0, concat_axis=1, tiled=True)
    grad_slab, grad_mine = unwind((grad_columns.astype(jnp.float32), jnp.zeros_like(slab_final)))
    grad_gated_cols = lax.all_to_all(
        grad_slab.astype(jnp.bfloat16), "ctx", split_axis=1, concat_axis=0, tiled=True
    )
    grad_gated_low = grad_gated_cols.T
    residue_terms = lax.all_gather(grad_mine, "ctx", axis=0, tiled=True)
    grad_gated = lax.optimization_barrier(grad_gated_low).astype(jnp.float32)
    grad_kshort = grad_gated * value_short
    grad_vshort = grad_gated * key_short
    heads = from_behind((grad_qshort[:span], grad_kshort[:span], grad_vshort[:span]), "ctx", -1)
    grad_query, taps_query = short_backward(
        grad_qshort, heads[0], query_proj, priors[0], short_taps[0]
    )
    grad_key, taps_key = short_backward(grad_kshort, heads[1], key_proj, priors[1], short_taps[1])
    grad_value, taps_value = short_backward(
        grad_vshort, heads[2], value_proj, priors[2], short_taps[2]
    )
    tap_terms = jnp.stack([taps_query, taps_key, taps_value])
    grad_taps = lax.psum(tap_terms.astype(jnp.bfloat16), "ctx").astype(jnp.float32)
    return (
        mixed,
        grad_query.astype(jnp.bfloat16),
        grad_key.astype(jnp.bfloat16),
        grad_value.astype(jnp.bfloat16),
        grad_taps,
        residue_terms,
    )


def solution(mesh):
    in_specs = (
        P("ctx", "tp"),
        P("ctx", "tp"),
        P("ctx", "tp"),
        P("ctx", "tp"),
        P(None, None, "tp"),
        P("tp", None),
        P("tp", None),
    )
    out_specs = (
        P("ctx", "tp"),
        P("ctx", "tp"),
        P("ctx", "tp"),
        P("ctx", "tp"),
        P(None, None, "tp"),
        P("tp", None),
    )
    return jax.shard_map(local, mesh=mesh, in_specs=in_specs, out_specs=out_specs, check_vma=False)
```

profile of v0, /device:TPU:0, one launch (start us, length us, event | category | flops | bytes accessed | tf_op | source)
XLA Modules:
  0.0 684.9 jit_solution(5089426856615203561)
XLA Ops:
  11.4 13.4 %fusion.39 = bf16[2048,1024]{0,1:T(8,128)(2,1)} fusion(bf16[1024,2048]{1,0:T(8,128)(2,1)} %param.9, bf16[2,2048]{1,0:T(2,128)(2,1)S(1)} %collective-permute-done.2, bf16[1024,2048]{1,0:T(8,128)(2,1)} %param.8, bf16[2,2048]{1,0:T(2,128)(2,1)S(1)} %collective-permute-done.1, f32[2048]{0:T(1024)S(1)} %bitcast.210, f32[2048]{0:T(1024)S(1)} %bitcast.212, ...), kind=kLoop, calls=%fused_computation.80 | loop fusion | flops 62914560 | bytes 12648448 | tf_op jit(solution)/shard_map/transpose | solution.py:97
  39.9 45.1 %all-to-all-done = bf16[8,256,1024]{2,1,0:T(8,128)(2,1)} async-done(((bf16[8,256,1024]{2,1,0:T(8,128)(2,1)}), bf16[8,256,1024]{2,1,0:T(8,128)(2,1)}, u32[]{:S(2)}, u32[]{:S(2)}) %all-to-all-start) | async-done | bytes 4194336 | tf_op jit(solution)/shard_map/all_to_all | solution.py:102
  91.5 7.3 %reshape.346 = bf16[16,16,64,128]{3,2,1,0:T(8,128)(2,1)} reshape(bf16[256,8,1024]{2,1,0:T(8,128)(2,1)} %copy.67) | data formatting | bytes 8388608 | tf_op jit(solution)/shard_map/jvp()/reshape | solution.py:42
  98.8 11.6 %fusion.65 = f32[16,16,64,16]{2,3,1,0:T(8,128)S(1)} fusion(bf16[16,16,64,128]{3,2,1,0:T(8,128)(2,1)} %reshape.346, f32[128]{0:T(128)S(1)} %iota_subtract_fusion.1, f32[16,16]{1,0:T(8,128)S(1)} %copy.68), kind=kOutput, calls=%fused_computation.151 | convolution fusion | flops 402685952 | bytes 5244416 | tf_op jit(solution)/shard_map/jvp(gms,gkns->nmgk)/dot_general | solution.py:44
  110.4 20.6 %slice.439 = f32[32,16,256]{0,1,2:T(8,128)} slice(f32[64,16,256]{0,1,2:T(8,128)S(1)} %bitcast.183), slice={[1:64:2], [0:16:1], [0:256:1]} | slice | bytes 1048576 | tf_op jit(solution)/shard_map/jvp()/slice | solution.py:49
  131.0 20.1 %slice.437 = f32[31,16,256]{0,1,2:T(8,128)} slice(f32[64,16,256]{0,1,2:T(8,128)S(1)} %bitcast.184), slice={[2:64:2], [0:16:1], [0:256:1]} | slice | bytes 1015808 | tf_op jit(solution)/shard_map/jvp()/slice | solution.py:49
  151.1 20.1 %slice.441 = f32[32,16,256]{0,1,2:T(8,128)} slice(f32[64,16,256]{0,1,2:T(8,128)S(1)} %bitcast.185), slice={[0:63:2], [0:16:1], [0:256:1]} | slice | bytes 1048576 | tf_op jit(solution)/shard_map/jvp()/slice | solution.py:49
  192.3 13.8 %fusion.68 = f32[16,64,16,128]{3,1,2,0:T(8,128)S(1)} fusion(f32[64,16,16,16]{0,1,3,2:T(8,128)S(1)} %bitcast.190, f32[128]{0:T(128)S(1)} %copy-done.30, f32[16,16]{1,0:T(8,128)S(1)} %copy-done.20, f32[16,16]{1,0:T(8,128)S(1)} %copy.68), kind=kOutput, calls=%fused_computation.154 | convolution fusion | flops 402718720 | bytes 9439744 | tf_op jit(solution)/shard_map/jvp(gmt,nmgk->gknt)/dot_general | solution.py:51
  206.5 8.8 %fusion.35 = bf16[16,16,64,128]{3,2,1,0:T(8,128)(2,1)} fusion(f32[16,64,16,128]{3,1,2,0:T(8,128)S(1)} %fusion.68, bf16[16,16,64,128]{3,2,1,0:T(8,128)(2,1)S(1)} %copy-done.5, f32[16]{0:T(128)S(1)} %copy-done.62, f32[16]{0:T(128)S(1)} %copy-done.69, f32[16]{0:T(128)S(1)} %copy-done.60, f32[16]{0:T(128)S(1)} %copy-done.71, f32[16]{0:T(128)S(1)} %copy-done.58, ...), kind=kOutput, calls=%fused_computation.68 | convolution fusion | flops 3238002688 | bytes 16861184 | tf_op jit(solution)/shard_map/jvp(gts,gkns->gknt)/dot_general | solution.py:43
  215.3 7.3 %convert_element_type.94 = bf16[256,8,1024]{2,1,0:T(8,128)(2,1)} reshape(bf16[16,16,64,128]{3,2,1,0:T(8,128)(2,1)} %fusion.35) | data formatting | bytes 8388608 | tf_op jit(solution)/shard_map/convert_element_type | solution.py:110
  236.8 46.0 %all-to-all-done.1 = bf16[256,8,1024]{2,0,1:T(8,128)(2,1)} async-done(((bf16[256,8,1024]{2,0,1:T(8,128)(2,1)}), bf16[256,8,1024]{2,0,1:T(8,128)(2,1)}, u32[]{:S(2)}, u32[]{:S(2)}) %all-to-all-start.1) | async-done | bytes 4194336 | tf_op jit(solution)/shard_map/all_to_all | solution.py:109
  282.9 6.6 copy.77
  289.5 21.5 %fusion.18 = (bf16[2048]{0:T(1024)(128)(2,1)}, bf16[2048]{0:T(1024)(128)(2,1)}, bf16[2048]{0:T(1024)(128)(2,1)}, bf16[2048,1024]{0,1:T(8,128)(2,1)}, bf16[1024,2048]{1,0:T(8,128)(2,1)}, /*index=5*/f32[1024,2048]{1,0:T(8,128)}) fusion(bf16[1024,2048]{1,0:T(8,128)(2,1)} %bitcast.192, bf16[1024,2048]{1,0:T(8,128)(2,1)} %param.10, bf16[1024,2048]{1,0:T(8,128)(2,1)} %param.7, ...), kind=kLoop, calls=%fused_computation.47 | loop fusion | flops 79685632 | bytes 29405184 | tf_op jit(solution)/shard_map/reduce_sum | solution.py:81
  317.4 52.6 %all_to_all.64 = bf16[8,256,1024]{2,1,0:T(8,128)(2,1)S(1)} all-to-all(bf16[8,256,1024]{2,1,0:T(8,128)(2,1)} %bitcast.194), channel_id=1, replica_groups=mesh['ctx'=8,'tp'=4] {'ctx'}, dimensions={0} | all-to-all | bytes 8388608 | tf_op jit(solution)/shard_map/all_to_all | solution.py:119
  374.4 7.3 %reshape.349 = bf16[16,16,64,128]{3,2,1,0:T(8,128)(2,1)} reshape(bf16[256,8,1024]{2,1,0:T(8,128)(2,1)} %copy.79) | data formatting | bytes 8388608 | tf_op jit(solution)/shard_map/transpose(jvp())/reshape | solution.py:57
  381.7 7.8 %fusion.46 = f32[64,16,16,16]{1,3,0,2:T(8,128)S(1)} fusion(bf16[16,16,64,128]{3,2,1,0:T(8,128)(2,1)} %reshape.349, f32[128]{0:T(128)S(1)} %copy-done.30, f32[16,16]{1,0:T(8,128)S(1)} %copy-done.20, f32[16,16]{1,0:T(8,128)S(1)} %copy.68), kind=kOutput, calls=%fused_computation.90 | convolution fusion | flops 402718720 | bytes 5245440 | tf_op jit(solution)/shard_map/transpose(jvp(gmt,nmgk->gknt))/dot_general | solution.py:51
  393.3 7.3 %copy.81 = f32[63,16,16,16]{0,3,2,1:T(8,128)} copy(f32[63,16,16,16]{1,3,0,2:T(8,128)} %split.47) | data formatting | bytes 2064384 | tf_op jit(solution)/shard_map/transpose(jvp())/split | solution.py:50
  413.2 8.1 %pad.238 = f32[32,16,256]{2,1,0:T(8,128)} pad(f32[15,16,256]{2,1,0:T(8,128)} %get-tuple-element.58, f32[]{:T(128)} %constant.10.clone.1), padding=2_1_1x0_0_0x0_0_0 | pad | bytes 770052 | tf_op jit(solution)/shard_map/transpose(jvp())/pad | solution.py:49
  429.1 15.6 %pad.269 = f32[64,16,256]{2,1,0:T(8,128)} pad(f32[32,16,256]{2,1,0:T(8,128)} %get-tuple-element.39, f32[]{:T(128)} %constant.10.clone.1), padding=0_1_1x0_0_0x0_0_0 | pad | bytes 1572868 | tf_op jit(solution)/shard_map/transpose(jvp())/pad | solution.py:49
  444.7 15.4 %pad.232 = f32[64,16,256]{2,1,0:T(8,128)} pad(f32[31,16,256]{2,1,0:T(8,128)} %get-tuple-element.54, f32[]{:T(128)} %constant.10.clone.1), padding=2_1_1x0_0_0x0_0_0 | pad | bytes 1556484 | tf_op jit(solution)/shard_map/transpose(jvp())/pad | solution.py:49
  460.1 11.0 %pad.268 = f32[64,16,256]{2,1,0:T(8,128)} pad(f32[32,16,256]{2,1,0:T(8,128)S(1)} %get-tuple-element.40, f32[]{:T(128)} %constant.10.clone.1), padding=1_0_1x0_0_0x0_0_0 | pad | bytes 1572868 | tf_op jit(solution)/shard_map/transpose(jvp())/pad | solution.py:49
  476.5 15.3 %fusion.63 = f32[16,16,64,128]{3,2,1,0:T(8,128)S(1)} fusion(f32[16,16,64,16]{2,3,1,0:T(8,128)} %bitcast.197, f32[128]{0:T(128)S(1)} %copy-done.33, f32[16,16]{1,0:T(8,128)S(1)} %copy.68), kind=kOutput, calls=%fused_computation.149 | convolution fusion | flops 402685952 | bytes 9438720 | tf_op jit(solution)/shard_map/transpose(jvp(gms,gkns->nmgk))/dot_general | solution.py:44
  492.1 8.8 %add_convert_fusion = bf16[16,16,64,128]{3,2,1,0:T(8,128)(2,1)} fusion(f32[16,16,64,128]{3,2,1,0:T(8,128)S(1)} %fusion.63, bf16[16,16,64,128]{3,2,1,0:T(8,128)(2,1)S(1)} %copy-done.2, f32[16]{0:T(128)S(1)} %copy-done.63, f32[16]{0:T(128)S(1)} %copy-done.70, f32[16]{0:T(128)S(1)} %copy-done.61, f32[16]{0:T(128)S(1)} %copy-done.72, f32[16]{0:T(128)S(1)} %copy-done.59, ...), kind=kOutput, calls=%fused_computation.69 | convolution fusion | flops 3238002688 | bytes 16861184 | tf_op jit(solution)/shard_map/transpose(jvp(gts,gkns->gknt))/dot_general | solution.py:43
  500.9 7.3 %convert_element_type.101 = bf16[256,8,1024]{2,1,0:T(8,128)(2,1)} reshape(bf16[16,16,64,128]{3,2,1,0:T(8,128)(2,1)} %add_convert_fusion) | data formatting | bytes 8388608 | tf_op jit(solution)/shard_map/convert_element_type | solution.py:122
  529.2 12.2 %fusion.14 = bf16[1024,2048]{1,0:T(8,128)(2,1)} fusion(f32[1024,2048]{1,0:T(8,128)} %get-tuple-element.53, f32[2,2048]{1,0:T(2,128)S(1)} %collective-permute-done.3, f32[2048]{0:T(1024)S(1)} %bitcast.217, f32[2048]{0:T(1024)S(1)} %bitcast.219, f32[2048]{0:T(1024)S(1)} %bitcast.215), kind=kLoop, calls=%fused_computation.43 | loop fusion | flops 16777216 | bytes 12623872 | tf_op jit(solution)/shard_map/convert_element_type | solution.py:141
  547.4 13.8 %fusion.56 = f32[16,16]{1,0:T(8,128)S(1)} fusion(f32[64,16,16,16]{3,1,0,2:T(8,128)} %copy.110, bf16[16,64,16,128]{3,1,2,0:T(8,128)(2,1)} %bitcast.187, f32[128]{0:T(128)S(1)} %copy-done.31, f32[16,16]{1,0:T(8,128)S(1)} %copy.68), kind=kOutput, calls=%fused_computation.96 | convolution fusion | flops 402751232 | bytes 5245440 | tf_op jit(solution)/shard_map/transpose(jvp(gmt,nmgk->gknt))/dot_general | solution.py:51
  561.3 46.5 %all_gather.3 = f32[128,16]{1,0:T(8,128)S(1)} all-gather(f32[16,16]{1,0:T(8,128)S(1)} %pad_add_fusion.8), channel_id=1, replica_groups=mesh['ctx'=8,'tp'=4] {'ctx'}, dimensions={0}, use_global_device_ids=true | all-gather | bytes 9216 | tf_op jit(solution)/shard_map/all_gather | solution.py:125
  608.5 6.7 copy.87
  615.2 13.7 %fusion.28 = (bf16[2048]{0:T(1024)(128)(2,1)S(1)}, bf16[2048]{0:T(1024)(128)(2,1)S(1)}, bf16[2048]{0:T(1024)(128)(2,1)S(1)}, f32[1024,2048]{1,0:T(8,128)S(1)}) fusion(bf16[1024,2048]{1,0:T(8,128)(2,1)} %param.9, bf16[2,2048]{1,0:T(2,128)(2,1)S(1)} %collective-permute-done.2, bf16[1024,2048]{1,0:T(8,128)(2,1)} %param.8, ...), kind=kLoop, calls=%fused_computation.57 | loop fusion | flops 65005568 | bytes 21024768 | tf_op jit(solution)/shard_map/reduce_sum | solution.py:81
  632.1 11.4 %fusion.23 = (bf16[2048]{0:T(1024)(128)(2,1)S(1)}, bf16[2048]{0:T(1024)(128)(2,1)S(1)}, bf16[2048]{0:T(1024)(128)(2,1)S(1)}, f32[1024,2048]{1,0:T(8,128)}, bf16[1024,2048]{1,0:T(8,128)(2,1)}) fusion(bf16[1024,2048]{1,0:T(8,128)(2,1)S(1)} %copy-done.1, bf16[2,2048]{1,0:T(2,128)(2,1)S(1)} %collective-permute-done.1, bf16[1024,2048]{1,0:T(8,128)(2,1)S(1)} %copy-done, ...), kind=kLoop, calls=%fused_computation.52 | loop fusion | flops 81782784 | bytes 33624064 | tf_op jit(solution)/shard_map/reduce_sum | solution.py:81
  645.7 26.3 %psum.7 = bf16[3,3,2048]{2,1,0:T(4,128)(2,1)S(1)} all-reduce(bf16[3,3,2048]{2,1,0:T(4,128)(2,1)S(1)} %pad_maximum_fusion.10), channel_id=1, replica_groups=mesh['ctx'=8,'tp'=4] {'ctx'}, use_global_device_ids=true, to_apply=%region_9.10 | all-reduce | flops 18432 | bytes 73728 | tf_op jit(solution)/shard_map/psum | solution.py:138
  672.7 12.0 %fusion.9 = bf16[1024,2048]{1,0:T(8,128)(2,1)} fusion(f32[1024,2048]{1,0:T(8,128)} %get-tuple-element.37, f32[2,2048]{1,0:T(2,128)S(1)} %collective-permute-done.4, f32[2048]{0:T(1024)S(1)} %bitcast.201, f32[2048]{0:T(1024)S(1)} %bitcast.204, f32[2048]{0:T(1024)S(1)} %bitcast.207), kind=kLoop, calls=%fused_computation.38 | loop fusion | flops 16777216 | bytes 12623872 | tf_op jit(solution)/shard_map/convert_element_type | solution.py:142
  (362 shorter events, 140.6 us)
Async XLA Ops:
  1.4 9.4 %collective-permute-start.2 = (bf16[2,2048]{1,0:T(2,128)(2,1)S(1)}, bf16[2,2048]{1,0:T(2,128)(2,1)S(1)}, u32[]{:S(2)}, u32[]{:S(2)}) collective-permute-start(bf16[2,2048]{1,0:T(2,128)(2,1)S(1)} %slice.399), channel_id=1, source_target_pairs={{0,4},{4,8},{8,12},{12,16},{16,20},{20,24},{24,28},{1,5},{5,9},{9,... | collective-permute-start | bytes 24584 | tf_op jit(solution)/shard_map/ppermute | solution.py:10
  4.6 6.2 collective-permute-start.1
  31.2 53.8 %all-to-all-start = ((bf16[8,256,1024]{2,1,0:T(8,128)(2,1)}), bf16[8,256,1024]{2,1,0:T(8,128)(2,1)}, u32[]{:S(2)}, u32[]{:S(2)}) async-start(bf16[8,256,1024]{2,1,0:T(8,128)(2,1)} %bitcast.193), calls=%async_computation | async-start | bytes 8388608 | tf_op jit(solution)/shard_map/all_to_all | solution.py:102
  37.8 61.0 %copy-start.32 = (f32[128]{0:T(128)}, f32[128]{0:T(128)S(1)}, u32[]{:S(2)}) copy-start(f32[128]{0:T(128)S(1)} %iota_subtract_fusion.1) | copy-start | bytes 1540
  229.1 60.4 %copy-start.14 = (f32[1,1,2048]{2,1,0:T(1,128)S(1)}, f32[1,1,2048]{2,1,0:T(1,128)}, u32[]{:S(2)}) copy-start(f32[1,1,2048]{2,1,0:T(1,128)} %get-tuple-element.66) | copy-start | bytes 24580
  229.1 60.4 %copy-start.16 = (f32[1,1,2048]{2,1,0:T(1,128)S(1)}, f32[1,1,2048]{2,1,0:T(1,128)}, u32[]{:S(2)}) copy-start(f32[1,1,2048]{2,1,0:T(1,128)} %get-tuple-element.71) | copy-start | bytes 24580
  229.1 60.4 %copy-start.18 = (f32[1,1,2048]{2,1,0:T(1,128)S(1)}, f32[1,1,2048]{2,1,0:T(1,128)}, u32[]{:S(2)}) copy-start(f32[1,1,2048]{2,1,0:T(1,128)} %get-tuple-element.72) | copy-start | bytes 24580
  229.1 53.8 %all-to-all-start.1 = ((bf16[256,8,1024]{2,0,1:T(8,128)(2,1)}), bf16[256,8,1024]{2,0,1:T(8,128)(2,1)}, u32[]{:S(2)}, u32[]{:S(2)}) async-start(bf16[256,8,1024]{2,0,1:T(8,128)(2,1)} %copy.76), calls=%async_computation.1 | async-start | bytes 8388608 | tf_op jit(solution)/shard_map/all_to_all | solution.py:109
  234.6 54.9 %collective-permute-start = (bf16[2,2048]{1,0:T(2,128)(2,1)S(1)}, bf16[2,2048]{1,0:T(2,128)(2,1)S(1)}, u32[]{:S(2)}, u32[]{:S(2)}) collective-permute-start(bf16[2,2048]{1,0:T(2,128)(2,1)S(1)} %slice.387), channel_id=1, source_target_pairs={{0,4},{4,8},{8,12},{12,16},{16,20},{20,24},{24,28},{1,5},{5,9},{9,... | collective-permute-start | bytes 24584 | tf_op jit(solution)/shard_map/ppermute | solution.py:10
  405.7 65.4 %slice-start = ((f32[32,16,256]{2,1,0:T(8,128)}), f32[1,16,256]{2,1,0:T(8,128)S(1)}, s32[]{:S(2)}) async-start(f32[32,16,256]{2,1,0:T(8,128)} %copy-done.7), calls=%async_computation.4 | async-start | bytes 32768 | tf_op jit(solution)/shard_map/transpose(jvp())/split | solution.py:49
  407.4 69.1 %copy-start.33 = (f32[128]{0:T(128)S(1)}, f32[128]{0:T(128)}, u32[]{:S(2)}) copy-start(f32[128]{0:T(128)} %copy-done.32) | copy-start | bytes 1540
  471.2 20.6 %copy-start.22 = (f32[128,128]{1,0:T(8,128)S(1)}, f32[128,128]{1,0:T(8,128)}, u32[]{:S(2)}) copy-start(f32[128,128]{1,0:T(8,128)} %fusion.86) | copy-start | bytes 196612
  471.2 20.6 %copy-start.29 = (pred[128,128]{1,0:T(8,128)(4,1)S(1)}, pred[128,128]{1,0:T(8,128)(4,1)}, u32[]{:S(2)}) copy-start(pred[128,128]{1,0:T(8,128)(4,1)} %fusion.87) | copy-start | bytes 49156
  471.2 20.6 %copy-start.35 = (f32[16]{0:T(128)S(1)}, f32[16]{0:T(128)}, u32[]{:S(2)}) copy-start(f32[16]{0:T(128)} %get-tuple-element.126) | copy-start | bytes 196
  471.2 20.6 %copy-start.37 = (f32[16]{0:T(128)S(1)}, f32[16]{0:T(128)}, u32[]{:S(2)}) copy-start(f32[16]{0:T(128)} %get-tuple-element.127) | copy-start | bytes 196
  471.2 20.6 %copy-start.39 = (f32[16]{0:T(128)S(1)}, f32[16]{0:T(128)}, u32[]{:S(2)}) copy-start(f32[16]{0:T(128)} %get-tuple-element.128) | copy-start | bytes 196
  471.2 20.6 %copy-start.41 = (f32[16]{0:T(128)S(1)}, f32[16]{0:T(128)}, u32[]{:S(2)}) copy-start(f32[16]{0:T(128)} %get-tuple-element.129) | copy-start | bytes 196
  471.2 20.6 %copy-start.43 = (f32[16]{0:T(128)S(1)}, f32[16]{0:T(128)}, u32[]{:S(2)}) copy-start(f32[16]{0:T(128)} %get-tuple-element.130) | copy-start | bytes 196
  471.3 20.6 %copy-start.45 = (f32[16]{0:T(128)S(1)}, f32[16]{0:T(128)}, u32[]{:S(2)}) copy-start(f32[16]{0:T(128)} %get-tuple-element.131) | copy-start | bytes 196
  471.3 20.6 %copy-start.47 = (f32[16]{0:T(128)S(1)}, f32[16]{0:T(128)}, u32[]{:S(2)}) copy-start(f32[16]{0:T(128)} %get-tuple-element.132) | copy-start | bytes 196
  471.3 20.6 %copy-start.49 = (f32[16]{0:T(128)S(1)}, f32[16]{0:T(128)}, u32[]{:S(2)}) copy-start(f32[16]{0:T(128)} %get-tuple-element.133) | copy-start | bytes 196
  471.3 20.6 %copy-start.51 = (f32[16]{0:T(128)S(1)}, f32[16]{0:T(128)}, u32[]{:S(2)}) copy-start(f32[16]{0:T(128)} %get-tuple-element.134) | copy-start | bytes 196
  471.3 20.6 %copy-start.53 = (f32[16]{0:T(128)S(1)}, f32[16]{0:T(128)}, u32[]{:S(2)}) copy-start(f32[16]{0:T(128)} %get-tuple-element.135) | copy-start | bytes 196
  471.3 20.6 %copy-start.55 = (f32[16]{0:T(128)S(1)}, f32[16]{0:T(128)}, u32[]{:S(2)}) copy-start(f32[16]{0:T(128)} %get-tuple-element.136) | copy-start | bytes 196
  471.3 20.6 %copy-start.57 = (f32[16]{0:T(128)S(1)}, f32[16]{0:T(128)}, u32[]{:S(2)}) copy-start(f32[16]{0:T(128)} %get-tuple-element.137) | copy-start | bytes 196
  471.3 20.6 %copy-start.59 = (f32[16]{0:T(128)S(1)}, f32[16]{0:T(128)}, u32[]{:S(2)}) copy-start(f32[16]{0:T(128)} %get-tuple-element.138) | copy-start | bytes 196
  471.3 20.6 %copy-start.61 = (f32[16]{0:T(128)S(1)}, f32[16]{0:T(128)}, u32[]{:S(2)}) copy-start(f32[16]{0:T(128)} %get-tuple-element.139) | copy-start | bytes 196
  471.3 20.6 %copy-start.63 = (f32[16]{0:T(128)S(1)}, f32[16]{0:T(128)}, u32[]{:S(2)}) copy-start(f32[16]{0:T(128)} %get-tuple-element.140) | copy-start | bytes 196
  514.7 93.8 %all-to-all-start.3 = ((bf16[256,8,1024]{2,0,1:T(8,128)(2,1)}), bf16[256,8,1024]{2,0,1:T(8,128)(2,1)}, u32[]{:S(2)}, u32[]{:S(2)}) async-start(bf16[256,8,1024]{2,0,1:T(8,128)(2,1)} %copy.86), calls=%async_computation.3 | async-start | bytes 8388608 | tf_op jit(solution)/shard_map/all_to_all | solution.py:121
  525.8 3.3 collective-permute-start.3
  628.9 3.1 collective-permute-start.5
  644.3 28.4 %collective-permute-start.4 = (f32[2,2048]{1,0:T(2,128)S(1)}, f32[2,2048]{1,0:T(2,128)S(1)}, u32[]{:S(2)}, u32[]{:S(2)}) collective-permute-start(f32[2,2048]{1,0:T(2,128)S(1)} %slice.519), channel_id=1, source_target_pairs={{4,0},{8,4},{12,8},{16,12},{20,16},{24,20},{28,24},{5,1},{9,5},{13... | collective-permute-start | bytes 49160 | tf_op jit(solution)/shard_map/ppermute | solution.py:10
  (77 other events, 1294.7 us)
where the time goes:
time: 694 us; the launch traced here: 685 us
  local copies, waits for them, and re-layouts  252 us (36%)
  blocking collectives  125 us (18%)
  other arithmetic  98.3 us (14%)
  waiting for transfers between devices  94.6 us (14%)
  matrix products  84.6 us (12%)
  starting transfers between devices  27.4 us (4%)
    pad x27, local copies, waits for them, and re-layouts, modal_conv(): lax.associative_scan(chain_combine, (factors, ends), axis=0)[1]  62.8 us
    slice x13, local copies, waits for them, and re-layouts, modal_conv(): lax.associative_scan(chain_combine, (factors, ends), axis=0)[1]  62.7 us
    all_to_all x1, blocking collectives, local(): lax.all_to_all(grad_cols_low, 'ctx', split_axis=0, concat_axis=1, tiled=T...  52.6 us
    reduce_sum x3, other arithmetic, short_backward(): tap_rows.append(jnp.sum(grad_out * window, axis=0))  46.6 us
    all_gather x1, blocking collectives, local(): residue_terms = lax.all_gather(grad_mine, 'ctx', axis=0, tiled=True)  46.5 us
    all_to_all x1, waiting for transfers between devices, local(): lax.all_to_all(slab_out.astype(jnp.bfloat16), 'ctx', split_axis=1, concat...  46 us
    all_to_all x1, waiting for transfers between devices, local(): lax.all_to_all(gated_cols_low, 'ctx', split_axis=0, concat_axis=1, tiled=...  45.1 us
    dot_general x3, matrix products, modal_conv(): jnp.einsum('gmt,nmgk->gknt', readin, before.reshape(count, modes, groups,...  35.4 us
  transfers between devices with their start and end apart: 9, of which 4 were waited for; matrix products, arithmetic and copies ran while one was open for 8% of the time, Pallas kernels for 0%

commit v1 on v0

v1 whole, which is shorter than its diff:
```python
import functools
import jax
import jax.numpy as jnp
from jax import lax
from jax.experimental import pallas as pl
from jax.experimental.pallas import tpu as pltpu
from jax.sharding import PartitionSpec as P

F32 = jnp.float32
BF16 = jnp.bfloat16
BLOCK = 128
LANES = 128
PAD = 8
HIGHEST = lax.Precision.HIGHEST


def dot(a, b, a_dim=1, b_dim=0, precision=None):
    return lax.dot_general(
        a, b, (((a_dim,), (b_dim,)), ((), ())), precision=precision, preferred_element_type=F32
    )


def iota(shape, axis):
    return lax.broadcasted_iota(jnp.int32, shape, axis)


def split(value):
    high = value.astype(BF16)
    return high, (value - high.astype(F32)).astype(BF16)


def eye():
    shape = (BLOCK, BLOCK)
    return (iota(shape, 0) == iota(shape, 1)).astype(F32).astype(BF16)


def fill_streams(streams, prior_ref, us, length):
    span = prior_ref.shape[0] // len(streams)
    for i, ref in enumerate(streams):
        us[i, PAD - span : PAD, :] = prior_ref[i * span : (i + 1) * span, :].astype(F32)
        us[i, PAD : PAD + length, :] = ref[...].astype(F32)


def windows(us, i, start, rows, taps):
    return [us[i, PAD + start - j : PAD + start - j + rows, :] for j in range(taps)]


def short(taps_ref, i, wins):
    taps = len(wins)
    total = taps_ref[i * taps : i * taps + 1, :] * wins[0]
    for j in range(1, taps):
        total = total + taps_ref[i * taps + j : i * taps + j + 1, :] * wins[j]
    return total


def states_kernel(
    sizes, me_ref, q_ref, k_ref, v_ref, c_ref, prior_ref, taps_ref, rate_col, rate_row,
    x_ref, h_ref, ef_ref, eb_ref, send_ref, us, gs, ls, af, ab,
):
    members, modes, taps, ctx = sizes
    length = q_ref.shape[0]
    count, groups = length // BLOCK, LANES // members
    width = groups * modes

    @pl.when(pl.program_id(0) == 0)
    def _():
        af[...] = jnp.zeros_like(af)
        ab[...] = jnp.zeros_like(ab)

    step = iota((width, BLOCK), 1).astype(F32)
    rate = rate_col[...]
    for table, array in ((af, jnp.exp(-rate * (BLOCK - 1.0 - step))), (ab, jnp.exp(-rate * step))):
        high, low = split(array)
        for g in range(groups):
            rows = slice(g * modes, (g + 1) * modes)
            lanes = slice(g * BLOCK, (g + 1) * BLOCK)
            table[g * modes : (g + 1) * modes, lanes] = high[rows]
            table[width + g * modes : width + (g + 1) * modes, lanes] = low[rows]
    fill_streams((q_ref, k_ref, v_ref), prior_ref, us, length)
    unit = eye()
    half = BLOCK // 2
    for n in range(count):
        for part in range(2):
            start = n * BLOCK + part * half
            rows = slice(start, start + half)
            query = short(taps_ref, 0, windows(us, 0, start, half, taps))
            key = short(taps_ref, 1, windows(us, 1, start, half, taps))
            value = short(taps_ref, 2, windows(us, 2, start, half, taps))
            gs[rows, :] = (key * value).astype(BF16)
            ls[rows, :] = (c_ref[rows, :].astype(F32) * query).astype(BF16)
        for source, target in ((gs, x_ref), (ls, h_ref)):
            turned = dot(unit, source[n * BLOCK : (n + 1) * BLOCK, :], 1, 1).astype(BF16)
            for g in range(groups):
                target[n * members : (n + 1) * members, g * BLOCK : (g + 1) * BLOCK] = turned[
                    g * members : (g + 1) * members
                ]
    decay = jnp.exp(-rate_row[0] * float(BLOCK))
    forward = dot(x_ref[...], af[...], 1, 1)
    forward = forward[:, :width] + forward[:, width:]
    backward = dot(h_ref[...], ab[...], 1, 1)
    backward = backward[:, :width] + backward[:, width:]
    ef_ref[...] = forward
    eb_ref[...] = backward
    last = jnp.zeros((members, width), F32)
    first = jnp.zeros((members, width), F32)
    for n in range(count):
        m = count - 1 - n
        last = decay * last + forward[n * members : (n + 1) * members]
        first = decay * first + backward[m * members : (m + 1) * members]
    me = me_ref[0]
    for j in range(ctx):
        send_ref[j] = jnp.where(j > me, last, first)


def inner_kernel(sizes, x_ref, h_ref, rate_col, res_col, y_ref, z_ref, grad_ref):
    members, modes, taps, ctx = sizes
    groups = LANES // members
    width = groups * modes
    step = iota((width, BLOCK), 1).astype(F32)
    rate, res = rate_col[...], res_col[...]
    rising = jnp.exp(-rate * (BLOCK - 1.0 - step))
    falling = res * jnp.exp(-rate * step)
    reverse = res * rising
    row, col = iota((BLOCK, BLOCK), 0), iota((BLOCK, BLOCK), 1)
    upper, lower, causal = col >= row, col <= row, row + col < BLOCK
    flip = (row + col == BLOCK - 1).astype(F32).astype(BF16)
    sums = []
    for g in range(groups):
        lanes = slice(g * BLOCK, (g + 1) * BLOCK)
        rows = slice(g * modes, (g + 1) * modes)
        taps_up = jnp.broadcast_to(jnp.sum(falling[rows], axis=0, keepdims=True), (BLOCK, BLOCK))
        taps_down = jnp.broadcast_to(jnp.sum(reverse[rows], axis=0, keepdims=True), (BLOCK, BLOCK))
        up = jnp.where(upper, pltpu.roll(taps_up, 0, 1, stride=1, stride_axis=0), 0.0).astype(BF16)
        down = jnp.where(lower, pltpu.roll(taps_down, 1, 1, stride=1, stride_axis=0), 0.0).astype(BF16)
        x, h = x_ref[:, lanes], h_ref[:, lanes]
        y_ref[:, lanes] = dot(x, up).astype(BF16)
        z_ref[:, lanes] = dot(h, down).astype(BF16)
        turned = dot(flip, h, 1, 1).astype(BF16)
        pairs = jnp.where(causal, dot(turned, x), 0.0)
        pairs = pltpu.roll(pairs, 0, 1, stride=1, stride_axis=0)
        sums.append(jnp.sum(pairs, axis=0, keepdims=True))
    crossed = dot(jnp.concatenate(sums, axis=0), rising, 1, 1, HIGHEST)
    own = iota((groups, width), 1) // modes == iota((groups, width), 0)
    grad_ref[0] = jnp.sum(jnp.where(own, crossed, 0.0), axis=0, keepdims=True)


def finish_kernel(
    sizes, me_ref, q_ref, k_ref, v_ref, c_ref, prior_ref, after_ref, taps_ref, rate_row, res_row,
    lag_ref, y_ref, z_ref, ef_ref, eb_ref, recv_ref, near_ref,
    mixed_ref, gq_ref, gk_ref, gv_ref, terms_ref, us, es, lo, gg,
):
    members, modes, taps, ctx = sizes
    length = q_ref.shape[0]
    count, groups = length // BLOCK, LANES // members
    width = groups * modes
    span = taps - 1
    rate, res = rate_row[0], res_row[0]
    me = me_ref[0]
    whole, decay = jnp.exp(-rate * float(length)), jnp.exp(-rate * float(BLOCK))
    ahead = jnp.zeros((members, width), F32)
    behind = jnp.zeros((members, width), F32)
    for i in range(ctx - 1):
        j = ctx - 1 - i
        ahead = jnp.where(i < me, whole * ahead + recv_ref[i], ahead)
        behind = jnp.where(j > me, whole * behind + recv_ref[j], behind)
    incoming = behind
    forward, backward = [], [None] * count
    for n in range(count):
        m = count - 1 - n
        forward.append(ahead)
        ahead = decay * ahead + ef_ref[n * members : (n + 1) * members, :]
        backward[m] = behind
        behind = decay * behind + eb_ref[m * members : (m + 1) * members, :]
    cross = forward[0] * eb_ref[0:members, :]
    for n in range(1, count):
        cross = cross + forward[n] * eb_ref[n * members : (n + 1) * members, :]
    grad_res = jnp.exp(-rate) * jnp.sum(cross, axis=0, keepdims=True) + lag_ref[0]

    step = iota((BLOCK, width), 0).astype(F32)
    unit = eye()
    lane_group = iota((members, width), 1) // modes
    for table, states, source, target in (
        (res * jnp.exp(-rate * (step + 1.0)), forward, y_ref, lo),
        (res * jnp.exp(-rate * (BLOCK - step)), backward, z_ref, gg),
    ):
        high, low = split(table)
        left = jnp.concatenate([unit, high, high, low], axis=1)
        for n in range(count):
            s_high = states[n].astype(BF16).astype(F32)
            s_low = states[n] - s_high
            rows = []
            for g in range(groups):
                own = lane_group == g
                wide = jnp.where(own, s_high, 0.0).astype(BF16)
                fine = jnp.where(own, s_low, 0.0).astype(BF16)
                piece = source[n * members : (n + 1) * members, g * BLOCK : (g + 1) * BLOCK]
                rows.append(jnp.concatenate([piece, wide, fine, wide], axis=1))
            right = jnp.concatenate(rows, axis=0)
            target[n * BLOCK : (n + 1) * BLOCK, :] = dot(left, right, 1, 1).astype(BF16)

    fill_streams((q_ref, k_ref, v_ref), prior_ref, us, length)
    rest = jnp.zeros((PAD - span, LANES), F32)
    head = after_ref[...].astype(F32)
    for i in range(3):
        us[i, PAD + length : 2 * PAD + length, :] = jnp.concatenate(
            [head[i * span : (i + 1) * span], rest], axis=0
        )
    cot = jnp.concatenate([head[3 * span : 4 * span], rest], axis=0)
    query = short(taps_ref, 0, windows(us, 0, length, PAD, taps))
    key = short(taps_ref, 1, windows(us, 1, length, PAD, taps))
    value = short(taps_ref, 2, windows(us, 2, length, PAD, taps))
    line = jnp.zeros((1, LANES), F32)
    second = iota((PAD, LANES), 0) == 1
    gated = (key * value).astype(BF16).astype(F32)
    grad_long = (cot * query).astype(BF16).astype(F32)
    gated_prev = jnp.where(second, jnp.concatenate([line, gated[:-1]], axis=0), 0.0)
    grad_prev = jnp.where(second, jnp.concatenate([line, grad_long[:-1]], axis=0), 0.0)
    order = iota((PAD, width), 0).astype(F32)

    def spread(state):
        return jnp.concatenate(
            [jnp.where(lane_group == g, state, 0.0) for g in range(groups)], axis=0
        )

    out = dot(res * jnp.exp(-rate * (order + 1.0)), spread(ahead), 1, 1, HIGHEST)
    out = out + near_ref[0:1, :] * gated + near_ref[1:2, :] * gated_prev
    out = out.astype(BF16).astype(F32)
    back = dot(res * jnp.exp(rate * order), spread(incoming), 1, 1, HIGHEST)
    back = back - near_ref[2:3, :] * grad_prev
    back = back.astype(BF16).astype(F32)
    for i, edge in enumerate((cot * out, back * value, back * key)):
        es[i, length : length + PAD, :] = edge

    part = BLOCK // 2
    sums = [jnp.zeros((8, LANES), F32) for _ in range(3 * taps)]
    for n in reversed(range(length // part)):
        start = n * part
        rows = slice(start, start + part)
        long_out, grad_gated = lo[rows, :].astype(F32), gg[rows, :].astype(F32)
        wins = [windows(us, i, start, part, taps) for i in range(3)]
        query, key, value = [short(taps_ref, i, wins[i]) for i in range(3)]
        mixed_ref[rows, :] = (query * long_out).astype(BF16)
        edges = (c_ref[rows, :].astype(F32) * long_out, grad_gated * value, grad_gated * key)
        for i, (edge, target) in enumerate(zip(edges, (gq_ref, gk_ref, gv_ref))):
            es[i, rows, :] = edge
            total = taps_ref[i * taps : i * taps + 1, :] * edge
            for j in range(1, taps):
                total = total + taps_ref[i * taps + j : i * taps + j + 1, :] * es[
                    i, start + j : start + j + part, :
                ]
            target[rows, :] = total.astype(BF16)
            for j in range(taps):
                product = edge * wins[i][j]
                sums[i * taps + j] = sums[i * taps + j] + jnp.sum(
                    product.reshape(part // 8, 8, LANES), axis=0
                )
    high, low = split(grad_res)
    lines = [jnp.sum(s, axis=0, keepdims=True) for s in sums]
    lines += [high.astype(F32), low.astype(F32)]
    lines.append(jnp.zeros((16 - len(lines), LANES), F32))
    terms = jnp.concatenate(lines, axis=0).astype(BF16)
    for j in range(ctx):
        terms_ref[j] = terms


def local(q, k, v, c, short_taps, residues, rates):
    length, wide = q.shape
    taps = short_taps.shape[1]
    span = taps - 1
    groups, modes = residues.shape
    members = wide // groups
    ctx = lax.axis_size("ctx")
    tiles = wide // LANES
    per = LANES // members
    rows = length // BLOCK * members
    lanes = per * BLOCK
    sizes = (members, modes, taps, ctx)
    me = lax.axis_index("ctx").astype(jnp.int32).reshape(1)
    prior = lax.ppermute(
        jnp.concatenate([q[length - span :], k[length - span :], v[length - span :]], axis=0),
        "ctx", [(i, i + 1) for i in range(ctx - 1)],
    )
    after = lax.ppermute(
        jnp.concatenate([q[:span], k[:span], v[:span], c[:span]], axis=0),
        "ctx", [(i + 1, i) for i in range(ctx - 1)],
    )
    tap_rows = short_taps.reshape(3 * taps, wide)
    rate_col, res_col = rates.reshape(groups * modes, 1), residues.reshape(groups * modes, 1)
    rate_row = rates.reshape(tiles, 1, per * modes)
    res_row = residues.reshape(tiles, 1, per * modes)
    near = jnp.stack(
        [
            jnp.sum(residues, axis=1),
            jnp.sum(residues * jnp.exp(-rates), axis=1),
            jnp.sum(residues * jnp.exp(rates), axis=1),
        ]
    )
    near = jnp.repeat(near, members, axis=1)

    smem = pl.BlockSpec(memory_space=pltpu.SMEM)
    stream = pl.BlockSpec((length, LANES), lambda i: (0, i))
    col = pl.BlockSpec((per * modes, 1), lambda i: (i, 0))
    row = pl.BlockSpec((1, 1, per * modes), lambda i: (i, 0, 0))
    turned = pl.BlockSpec((rows, lanes), lambda i: (i, 0))
    ends = pl.BlockSpec((rows, per * modes), lambda i: (i, 0))
    swap = pl.BlockSpec((ctx, members, per * modes), lambda i: (0, i, 0))

    def strip(n):
        return pl.BlockSpec((n, LANES), lambda i: (0, i))

    turned_shape = jax.ShapeDtypeStruct((tiles * rows, lanes), BF16)
    ends_shape = jax.ShapeDtypeStruct((tiles * rows, per * modes), F32)
    x, h, ef, eb, send = pl.pallas_call(
        functools.partial(states_kernel, sizes),
        grid=(tiles,),
        in_specs=[smem, stream, stream, stream, stream, strip(3 * span), strip(3 * taps), col, row],
        out_specs=[turned, turned, ends, ends, swap],
        out_shape=[
            turned_shape, turned_shape, ends_shape, ends_shape,
            jax.ShapeDtypeStruct((ctx, tiles * members, per * modes), F32),
        ],
        scratch_shapes=[
            pltpu.VMEM((3, PAD + length, LANES), F32),
            pltpu.VMEM((length, LANES), BF16),
            pltpu.VMEM((length, LANES), BF16),
            pltpu.VMEM((2 * per * modes, lanes), BF16),
            pltpu.VMEM((2 * per * modes, lanes), BF16),
        ],
        cost_estimate=pl.CostEstimate(flops=4 * 10**9, bytes_accessed=26 * 10**6, transcendentals=0),
        name="states",
    )(me, q, k, v, c, prior, tap_rows, rate_col, rate_row)
    recv = lax.all_to_all(send, "ctx", split_axis=0, concat_axis=0, tiled=True)
    y, z, lag = pl.pallas_call(
        functools.partial(inner_kernel, sizes),
        grid=(tiles,),
        in_specs=[turned, turned, col, col],
        out_specs=[turned, turned, row],
        out_shape=[
            turned_shape, turned_shape, jax.ShapeDtypeStruct((tiles, 1, per * modes), F32),
        ],
        cost_estimate=pl.CostEstimate(flops=4 * 10**9, bytes_accessed=17 * 10**6, transcendentals=0),
        name="inner",
    )(x, h, rate_col, res_col)
    big = jax.ShapeDtypeStruct((length, wide), BF16)
    mixed, gq, gk, gv, terms = pl.pallas_call(
        functools.partial(finish_kernel, sizes),
        grid=(tiles,),
        in_specs=[
            smem, stream, stream, stream, stream, strip(3 * span), strip(4 * span), strip(3 * taps),
            row, row, row, turned, turned, ends, ends, swap, strip(3),
        ],
        out_specs=[
            stream, stream, stream, stream,
            pl.BlockSpec((ctx, 16, LANES), lambda i: (0, 0, i)),
        ],
        out_shape=[big, big, big, big, jax.ShapeDtypeStruct((ctx, 16, wide), BF16)],
        scratch_shapes=[
            pltpu.VMEM((3, 2 * PAD + length, LANES), F32),
            pltpu.VMEM((3, PAD + length, LANES), F32),
            pltpu.VMEM((length, LANES), BF16),
            pltpu.VMEM((length, LANES), BF16),
        ],
        cost_estimate=pl.CostEstimate(flops=8 * 10**9, bytes_accessed=42 * 10**6, transcendentals=0),
        name="finish",
    )(me, q, k, v, c, prior, after, tap_rows, rate_row, res_row, lag, y, z, ef, eb, recv, near)
    total = jnp.sum(
        lax.all_to_all(terms, "ctx", split_axis=0, concat_axis=0, tiled=True).astype(F32), axis=0
    )
    count = 3 * taps
    grad_taps = total[:count].reshape(3, taps, wide)
    grad_res = (total[count] + total[count + 1]).reshape(groups, modes)
    return mixed, gq, gk, gv, grad_taps, grad_res


def solution(mesh):
    stream = P("ctx", "tp")
    return jax.shard_map(
        local,
        mesh=mesh,
        in_specs=(stream, stream, stream, stream, P(None, None, "tp"), P("tp", None), P("tp", None)),
        out_specs=(stream, stream, stream, stream, P(None, None, "tp"), P("tp", None)),
        check_vma=False,
    )
```

time: 694 us -> 124 us (0.18); the launches traced: 685 us -> 123 us
  local copies, waits for them, and re-layouts: 252 us -> 12.5 us
  blocking collectives: 125 us -> 15.3 us
  other arithmetic: 98.3 us -> 0.22 us
  waiting for transfers between devices: 94.6 us -> 0.01 us
  Pallas kernels: 0 us -> 86 us
  matrix products: 84.6 us -> 0 us
  starting transfers between devices: 27.4 us -> 8.7 us
    all_to_all x3 -> x1, waiting for transfers between devices: 91.2 us -> 0.01 us  [local(): recv = lax.all_to_all(send, 'ctx', split_axis=0, concat_axis=0, tiled=True)]
    pallas_call x0 -> x3, Pallas kernels: none -> 86 us  [the longest x1 32.4 us: local(): pl.pallas_call(functools.partial(inner_kernel, sizes), grid=(tiles,), in_...]
    dot_general x8 -> x0, matrix products: 84.6 us -> none  [the longest x3 35.4 us: modal_conv(): jnp.einsum('gmt,nmgk->gknt', readin, before.reshape(count, modes, groups,...]
    slice x21 -> x4, local copies, waits for them, and re-layouts: 68.8 us -> 1.64 us  [the longest x1 0.84 us: local(): q[:span]]
    pad x27 -> x0, local copies, waits for them, and re-layouts: 62.8 us -> none  [modal_conv(): lax.associative_scan(chain_combine, (factors, ends), axis=0)[1]]
    reduce_sum x3 -> x2, other arithmetic: 46.6 us -> 0.1 us  [the longest x1 0.07 us: local(): jnp.sum(lax.all_to_all(terms, 'ctx', split_axis=0, concat_axis=0, tiled=T...]
    all_gather x1 -> x0, blocking collectives: 46.5 us -> none  [local(): residue_terms = lax.all_gather(grad_mine, 'ctx', axis=0, tiled=True)]
    all_to_all x1, blocking collectives: 52.6 us -> 15.3 us  [local(): lax.all_to_all(terms, 'ctx', split_axis=0, concat_axis=0, tiled=True)]
  transfers between devices with their start and end apart: 9 -> 3, of which waited for: 4 -> 0; matrix products, arithmetic and copies ran while one was open for 8% -> 6% of each run, Pallas kernels for 0% -> 26%
where the time goes in v1:
time: 124 us; the launch traced here: 123 us
  Pallas kernels  86 us (69%)
  blocking collectives  15.3 us (12%)
  local copies, waits for them, and re-layouts  12.5 us (10%)
  starting transfers between devices  8.7 us (7%)
    pallas_call x1, Pallas kernels, local(): pl.pallas_call(functools.partial(inner_kernel, sizes), grid=(tiles,), in_...  32.4 us
    pallas_call x1, Pallas kernels, local(): pl.pallas_call(functools.partial(finish_kernel, sizes), grid=(tiles,), in...  32 us
    pallas_call x1, Pallas kernels, local(): pl.pallas_call(functools.partial(states_kernel, sizes), grid=(tiles,), in...  21.7 us
    all_to_all x1, blocking collectives, local(): lax.all_to_all(terms, 'ctx', split_axis=0, concat_axis=0, tiled=True)  15.3 us
    all_to_all x1, starting transfers between devices, local(): recv = lax.all_to_all(send, 'ctx', split_axis=0, concat_axis=0, tiled=True)  5.01 us
    unnamed x13, local copies, waits for them, and re-layouts  3.16 us
  transfers between devices with their start and end apart: 3, of which 0 were waited for; matrix products, arithmetic and copies ran while one was open for 6% of the time, Pallas kernels for 26%

profile of v1, /device:TPU:0, one launch (start us, length us, event | category | flops | bytes accessed | tf_op | source)
XLA Modules:
  0.0 123.5 jit_solution(10327010110820434121)
XLA Ops:
  0.6 0.8 fusion.3
  1.4 0.8 fusion.1
  2.3 2.4 %collective-permute-start = (bf16[6,2048]{1,0:T(8,128)(2,1)S(1)}, bf16[6,2048]{1,0:T(8,128)(2,1)S(1)}, u32[]{:S(2)}, u32[]{:S(2)}) collective-permute-start(bf16[6,2048]{1,0:T(8,128)(2,1)S(1)} %pad_maximum_fusion), channel_id=1, source_target_pairs={{0,4},{4,8},{8,12},{12,16},{16,20},{20,24},{24,28},{1,5},{5,9},{9,... | collective-permute-start | bytes 73736 | tf_op jit(solution)/shard_map/ppermute | solution.py:279
  4.7 0.8 copy.17
  5.5 0.7 reshape.42
  6.2 1.6 %reshape.48.rate_col = f32[2048,1]{1,0:T(8,128)} reshape(f32[128,16]{1,0:T(8,128)S(1)} %copy.17) | data formatting | bytes 16384 | tf_op jit(solution)/shard_map/reshape | solution.py:288
  7.8 1.6 %reshape.41.taps_ref = f32[9,2048]{1,0:T(8,128)} reshape(f32[3,3,2048]{2,1,0:T(4,128)} %param.11) | data formatting | bytes 147456 | tf_op jit(solution)/shard_map/reshape | solution.py:287
  9.3 0.0 collective-permute-done.prior_ref
  9.3 0.6 copy-done.1
  10.0 21.7 %states.1 = (bf16[2048,1024]{1,0:T(8,128)(2,1)}, bf16[2048,1024]{1,0:T(8,128)(2,1)}, f32[2048,128]{1,0:T(8,128)}, f32[2048,128]{1,0:T(8,128)}, f32[8,256,128]{2,1,0:T(8,128)}) custom-call(s32[1]{0:T(128)} %bitcast.me_ref, bf16[1024,2048]{1,0:T(8,128)(2,1)} %q_ref.3, bf16[1024,2048]{1,0:T(8,128)(2,1)} %k_ref.3, bf16[1024,2048]{1,0:T(8,128)(2,1)} %v_ref.3, ...), custom_call_target="tpu_custom_call" | custom-call | flops 4000000000 | bytes 26000000 | tf_op jit(solution)/shard_map/states/pallas_call | solution.py:313
  31.6 5.0 %all-to-all-start = ((f32[8,256,128]{2,1,0:T(8,128)}), f32[8,256,128]{2,1,0:T(8,128)S(1)}, u32[]{:S(2)}, u32[]{:S(2)}) async-start(f32[8,256,128]{2,1,0:T(8,128)} %get-tuple-element.26), calls=%async_computation | async-start | bytes 2097152 | tf_op jit(solution)/shard_map/all_to_all | solution.py:332
  36.6 0.0 slice-done
  36.7 1.3 %collective-permute-start.1 = (bf16[8,2048]{1,0:T(8,128)(2,1)S(1)}, bf16[8,2048]{1,0:T(8,128)(2,1)S(1)}, u32[]{:S(2)}, u32[]{:S(2)}) collective-permute-start(bf16[8,2048]{1,0:T(8,128)(2,1)S(1)} %pad_maximum_fusion.1), channel_id=1, source_target_pairs={{4,0},{8,4},{12,8},{16,12},{20,16},{24,20},{28,24},{5,1},{9,5},{13... | collective-permute-start | bytes 98312 | tf_op jit(solution)/shard_map/ppermute | solution.py:283
  38.0 0.0 copy-done.3
  38.0 0.1 copy.18
  38.1 0.7 reshape.43
  38.8 1.6 %reshape.49.res_col = f32[2048,1]{1,0:T(8,128)} reshape(f32[128,16]{1,0:T(8,128)S(1)} %copy.18) | data formatting | bytes 16384 | tf_op jit(solution)/shard_map/reshape | solution.py:288
  40.3 0.0 copy-done.2
  40.4 0.1 broadcast_in_dim.3
  40.5 0.7 reshape.46.near_ref
  41.2 32.4 %inner.1 = (bf16[2048,1024]{1,0:T(8,128)(2,1)}, bf16[2048,1024]{1,0:T(8,128)(2,1)}, f32[16,1,128]{2,1,0:T(1,128)}) custom-call(bf16[2048,1024]{1,0:T(8,128)(2,1)} %get-tuple-element.19.x_ref, bf16[2048,1024]{1,0:T(8,128)(2,1)} %get-tuple-element.20.h_ref, f32[2048,1]{1,0:T(8,128)} %reshape.48.rate_col, f32[2048,1]{1,0:T(8,128)} %reshape.49.res_col), custom_call_target="tpu_custom_call" | custom-call | flops 4000000000 | bytes 17000000 | tf_op jit(solution)/shard_map/inner/pallas_call | solution.py:333
  73.7 0.0 collective-permute-done.1.after_ref
  73.7 0.0 all-to-all-done.recv_ref
  73.7 0.0 copy-start
  73.7 0.6 copy-done.4
  74.3 0.4 copy-done
  74.6 32.0 %finish.1 = (bf16[1024,2048]{1,0:T(8,128)(2,1)}, bf16[1024,2048]{1,0:T(8,128)(2,1)}, bf16[1024,2048]{1,0:T(8,128)(2,1)}, bf16[1024,2048]{1,0:T(8,128)(2,1)}, bf16[8,16,2048]{2,1,0:T(8,128)(2,1)}) custom-call(s32[1]{0:T(128)} %bitcast.me_ref, bf16[1024,2048]{1,0:T(8,128)(2,1)} %q_ref.3, bf16[1024,2048]{1,0:T(8,128)(2,1)} %k_ref.3, bf16[1024,2048]{1,0:T(8,128)(2,1)} %v_ref.3, ...), custom_call_target="tpu_custom_call" | custom-call | flops 8000000000 | bytes 42000000 | tf_op jit(solution)/shard_map/finish/pallas_call | solution.py:345
  106.6 15.3 %all_to_all.10 = bf16[8,16,2048]{2,1,0:T(8,128)(2,1)S(1)} all-to-all(bf16[8,16,2048]{2,1,0:T(8,128)(2,1)} %get-tuple-element.31), channel_id=1, replica_groups=mesh['ctx'=8,'tp'=4] {'ctx'}, dimensions={0} | all-to-all | bytes 1048576 | tf_op jit(solution)/shard_map/all_to_all | solution.py:367
  121.9 0.1 convert_reduce_fusion
  122.1 0.1 add.8
  122.1 0.7 copy.27
  122.8 0.7 reshape.47
  (10 shorter events, 0.2 us)
Async XLA Ops:
  2.3 7.0 %collective-permute-start = (bf16[6,2048]{1,0:T(8,128)(2,1)S(1)}, bf16[6,2048]{1,0:T(8,128)(2,1)S(1)}, u32[]{:S(2)}, u32[]{:S(2)}) collective-permute-start(bf16[6,2048]{1,0:T(8,128)(2,1)S(1)} %pad_maximum_fusion), channel_id=1, source_target_pairs={{0,4},{4,8},{8,12},{12,16},{16,20},{20,24},{24,28},{1,5},{5,9},{9,... | collective-permute-start | bytes 73736 | tf_op jit(solution)/shard_map/ppermute | solution.py:279
  9.3 0.6 copy-start.1
  10.0 26.7 %slice-start = ((bf16[1024,2048]{1,0:T(8,128)(2,1)}), bf16[2,2048]{1,0:T(2,128)(2,1)S(1)}, s32[]{:S(2)}) async-start(bf16[1024,2048]{1,0:T(8,128)(2,1)} %c_ref.3), calls=%async_computation.2 | async-start | bytes 16384 | tf_op jit(solution)/shard_map/slice | solution.py:284
  10.0 28.0 %copy-start.3 = (f32[128,16]{0,1:T(8,128)S(1)}, f32[128,16]{0,1:T(8,128)}, u32[]{:S(2)}) copy-start(f32[128,16]{0,1:T(8,128)} %param.12) | copy-start | bytes 24580
  10.0 30.4 %copy-start.2 = (f32[128,16]{0,1:T(8,128)S(1)}, f32[128,16]{0,1:T(8,128)}, u32[]{:S(2)}) copy-start(f32[128,16]{0,1:T(8,128)} %param.13) | copy-start | bytes 24580
  31.6 42.0 %all-to-all-start = ((f32[8,256,128]{2,1,0:T(8,128)}), f32[8,256,128]{2,1,0:T(8,128)S(1)}, u32[]{:S(2)}, u32[]{:S(2)}) async-start(f32[8,256,128]{2,1,0:T(8,128)} %get-tuple-element.26), calls=%async_computation | async-start | bytes 2097152 | tf_op jit(solution)/shard_map/all_to_all | solution.py:332
  36.7 37.0 %collective-permute-start.1 = (bf16[8,2048]{1,0:T(8,128)(2,1)S(1)}, bf16[8,2048]{1,0:T(8,128)(2,1)S(1)}, u32[]{:S(2)}, u32[]{:S(2)}) collective-permute-start(bf16[8,2048]{1,0:T(8,128)(2,1)S(1)} %pad_maximum_fusion.1), channel_id=1, source_target_pairs={{4,0},{8,4},{12,8},{16,12},{20,16},{24,20},{28,24},{5,1},{9,5},{13... | collective-permute-start | bytes 98312 | tf_op jit(solution)/shard_map/ppermute | solution.py:283
  73.7 0.6 copy-start.4
  73.7 1.0 copy-start

commit v2 on v1

v2 whole, which is shorter than its diff:
```python
import functools
import jax
import jax.numpy as jnp
from jax import lax
from jax.experimental import pallas as pl
from jax.experimental.pallas import tpu as pltpu
from jax.sharding import PartitionSpec as P

F32 = jnp.float32
BF16 = jnp.bfloat16
BLOCK = 128
LANES = 128
TILES = 2
PAD = 8
PART = 64
KEPT = (0, 1, 2)


def dot(a, b, a_dim=1, b_dim=0, precision=None):
    return lax.dot_general(
        a, b, (((a_dim,), (b_dim,)), ((), ())), precision=precision, preferred_element_type=F32
    )


def iota(shape, axis):
    return lax.broadcasted_iota(jnp.int32, shape, axis)


def split(value):
    high = value.astype(BF16)
    return high, (value - high.astype(F32)).astype(BF16)


def mask(condition):
    return condition.astype(F32).astype(BF16)


def eye():
    shape = (BLOCK, BLOCK)
    return mask(iota(shape, 0) == iota(shape, 1))


def fine_dot(a, b, a_dim=1, b_dim=0):
    rows = a.shape[0]
    a_high, a_low = split(a)
    b_high, b_low = split(b)
    wide = dot(jnp.concatenate([a_high, a_low], axis=0), b_high, a_dim, b_dim)
    return wide[:rows] + (wide[rows:] + dot(a_high, b_low, a_dim, b_dim))


def as_row(value):
    groups, modes = value.shape
    width = groups * modes
    pick = mask(iota((modes, width), 1) % modes == iota((modes, width), 0))
    high = value.astype(BF16).astype(F32)
    middle = (value - high).astype(BF16).astype(F32)
    low = value - high - middle
    wide = dot(jnp.concatenate([high, middle, low], axis=0).astype(BF16), pick)
    own = iota((3 * groups, width), 1) // modes == iota((3 * groups, width), 0) % groups
    wide = jnp.where(own, wide, 0.0)
    parts = [
        jnp.sum(wide[i * groups : (i + 1) * groups], axis=0, keepdims=True) for i in range(3)
    ]
    return parts[0] + (parts[1] + parts[2])


def powers(rate_row, first, down):
    width = rate_row.shape[1]
    row = iota((8, width), 0).astype(F32)
    lag = 7.0 - row if down else row
    part = jnp.exp(-rate_row * (lag + first))
    factor = jnp.exp(-rate_row * 8.0)
    parts = [part]
    for _ in range(BLOCK // 8 - 1):
        parts.append(parts[-1] * factor)
    return jnp.concatenate(parts[::-1] if down else parts, axis=0)


def fill_streams(streams, prior_ref, us, length):
    span = prior_ref.shape[0] // len(streams)
    for i, ref in enumerate(streams):
        us[i, PAD - span : PAD, :] = prior_ref[i * span : (i + 1) * span, :].astype(F32)
        us[i, PAD : PAD + length, :] = ref[...].astype(F32)


def windows(us, i, start, rows, taps):
    return [us[i, PAD + start - j : PAD + start - j + rows, :] for j in range(taps)]


def short(taps_ref, i, wins):
    total = taps_ref[i, 0:1, :] * wins[0]
    for j in range(1, len(wins)):
        total = total + taps_ref[i, j : j + 1, :] * wins[j]
    return total


def states_tile(
    sizes, me, q_ref, k_ref, v_ref, c_ref, prior_ref, taps_ref, rates,
    x_ref, h_ref, ef_ref, eb_ref, send_ref, short_refs, us, gs, ls, af, ab,
):
    members, modes, taps, ctx = sizes
    length = q_ref.shape[0]
    count, groups = length // BLOCK, LANES // members
    width = groups * modes
    unit = eye()
    rate = as_row(rates)
    fill_streams((q_ref, k_ref, v_ref), prior_ref, us, length)
    half = BLOCK // 2
    for n in range(count):
        for part in range(2):
            start = n * BLOCK + part * half
            rows = slice(start, start + half)
            shorts = [short(taps_ref, i, windows(us, i, start, half, taps)) for i in range(3)]
            for i, ref in short_refs.items():
                ref[rows, :] = shorts[i].astype(BF16)
            gs[rows, :] = (shorts[1] * shorts[2]).astype(BF16)
            ls[rows, :] = (c_ref[rows, :].astype(F32) * shorts[0]).astype(BF16)
        if n % 2 == 0 and n + 1 < count:
            continue
        blocks = [n - 1, n] if n % 2 else [n]
        for source, target in ((gs, x_ref), (ls, h_ref)):
            rows = slice(blocks[0] * BLOCK, (n + 1) * BLOCK)
            turned = dot(unit, source[rows, :], 1, 1).astype(BF16)
            for at, m in enumerate(blocks):
                for g in range(groups):
                    target[m * members : (m + 1) * members, g * BLOCK : (g + 1) * BLOCK] = turned[
                        g * members : (g + 1) * members, at * BLOCK : (at + 1) * BLOCK
                    ]
        if n == 1:
            for table, array in ((af, powers(rate, 0.0, True)), (ab, powers(rate, 0.0, False))):
                both = jnp.concatenate(split(array), axis=1)
                lane_group = iota(both.shape, 1) % width // modes
                for g in range(groups):
                    table[g * BLOCK : (g + 1) * BLOCK, :] = both * mask(lane_group == g)
    decay = jnp.exp(-rate * float(BLOCK))
    forward = dot(x_ref[...], af[...])
    forward = forward[:, :width] + forward[:, width:]
    backward = dot(h_ref[...], ab[...])
    backward = backward[:, :width] + backward[:, width:]
    ef_ref[...] = forward
    eb_ref[...] = backward
    last = jnp.zeros((members, width), F32)
    first = jnp.zeros((members, width), F32)
    for n in range(count):
        m = count - 1 - n
        last = decay * last + forward[n * members : (n + 1) * members]
        first = decay * first + backward[m * members : (m + 1) * members]
    for j in range(ctx):
        send_ref[j] = jnp.where(j > me, last, first)


def states_kernel(sizes, *refs):
    members, modes, taps, ctx = sizes
    me_ref, q_ref, k_ref, v_ref, c_ref, prior_ref, taps_ref, rate_ref = refs[:8]
    x_ref, h_ref, ef_ref, eb_ref, send_ref = refs[8:13]
    kept = refs[13 : 13 + len(KEPT)]
    us, gs, ls, af, ab = refs[13 + len(KEPT) :]
    groups = LANES // members
    rows = x_ref.shape[0] // TILES
    for t in range(TILES):
        lanes, part = pl.ds(t * LANES, LANES), pl.ds(t * rows, rows)
        states_tile(
            sizes, me_ref[0],
            *[r.at[:, lanes] for r in (q_ref, k_ref, v_ref, c_ref, prior_ref)],
            taps_ref.at[:, :, lanes], rate_ref[t * groups : (t + 1) * groups, :],
            *[r.at[part, :] for r in (x_ref, h_ref, ef_ref, eb_ref)],
            send_ref.at[:, pl.ds(t * members, members), :],
            {i: r.at[:, lanes] for i, r in zip(KEPT, kept)},
            us.at[t], gs.at[t], ls.at[t], af.at[t], ab.at[t],
        )


def pairs_tile(sizes, x_ref, h_ref, rates, grad_ref):
    members, modes, taps, ctx = sizes
    groups = LANES // members
    width = groups * modes
    rate = as_row(rates)
    row, col = iota((BLOCK, BLOCK), 0), iota((BLOCK, BLOCK), 1)
    causal = row + col < BLOCK
    flip = mask(row + col == BLOCK - 1)
    sums = []
    for p in range(0, groups, 2):
        pair = range(p, min(p + 2, groups))
        stack = [h_ref[:, g * BLOCK : (g + 1) * BLOCK] for g in pair]
        turned = dot(flip, jnp.concatenate(stack, axis=0), 1, 1).astype(BF16)
        for at, g in enumerate(pair):
            x = x_ref[:, g * BLOCK : (g + 1) * BLOCK]
            rows = x.shape[0]
            pairs = jnp.where(causal, dot(turned[:, at * rows : (at + 1) * rows], x), 0.0)
            total = pairs[0:8]
            for i in range(1, BLOCK // 8):
                total = total + pltpu.roll(pairs[8 * i : 8 * i + 8], 8 * i, 1)
            sums.append(pltpu.roll(total, 0, 1, stride=1, stride_axis=0))
    crossed = fine_dot(jnp.concatenate(sums, axis=0), powers(rate, 0.0, True))
    shape = (8 * groups, width)
    grad_ref[...] = jnp.sum(
        jnp.where(iota(shape, 1) // modes == iota(shape, 0) // 8, crossed, 0.0), axis=0, keepdims=True
    )


def pairs_kernel(sizes, x_ref, h_ref, rate_ref, grad_ref):
    groups = LANES // sizes[0]
    rows = x_ref.shape[0] // TILES
    for t in range(TILES):
        part, own = pl.ds(t * rows, rows), slice(t * groups, (t + 1) * groups)
        pairs_tile(sizes, x_ref.at[part, :], h_ref.at[part, :], rate_ref[own, :], grad_ref.at[t])


def conv_steps(
    sizes, length, me, rates, residues, lag_ref, x_ref, h_ref, ef_ref, eb_ref, recv_ref,
    ts, rs, turn, note,
):
    members, modes, taps, ctx = sizes
    count, groups = length // BLOCK, LANES // members
    width = groups * modes
    rate, res = as_row(rates), as_row(residues)
    states, lefts, own = [], {}, {}

    def prepare():
        whole, decay = jnp.exp(-rate * float(length)), jnp.exp(-rate * float(BLOCK))
        ahead = jnp.zeros((members, width), F32)
        behind = jnp.zeros((members, width), F32)
        for i in range(ctx - 1):
            j = ctx - 1 - i
            ahead = jnp.where(i < me, whole * ahead + recv_ref[i], ahead)
            behind = jnp.where(j > me, whole * behind + recv_ref[j], behind)
        incoming = behind
        forward, backward = [], [None] * count
        for n in range(count):
            m = count - 1 - n
            forward.append(ahead)
            ahead = decay * ahead + ef_ref[n * members : (n + 1) * members, :]
            backward[m] = behind
            behind = decay * behind + eb_ref[m * members : (m + 1) * members, :]
        cross = forward[0] * eb_ref[0:members, :]
        for n in range(1, count):
            cross = cross + forward[n] * eb_ref[n * members : (n + 1) * members, :]
        states.extend((forward, backward))

        order = iota((PAD, width), 0).astype(F32)
        lane_group = iota((members, width), 1) // modes
        channel_own = iota((groups, LANES), 1) // members == iota((groups, LANES), 0)

        def spread(state):
            return jnp.concatenate(
                [jnp.where(lane_group == g, state, 0.0) for g in range(groups)], axis=0
            )

        def near(shift):
            sums = jnp.sum(residues * jnp.exp(-rates * shift), axis=1, keepdims=True)
            return jnp.sum(jnp.where(channel_own, sums, 0.0), axis=0, keepdims=True)

        note[0] = fine_dot(res * jnp.exp(-rate * (order + 1.0)), spread(ahead), 1, 1)
        note[1] = fine_dot(res * jnp.exp(rate * order), spread(incoming), 1, 1)
        note[2, 0:1, :] = near(0.0)
        note[2, 1:2, :] = near(1.0)
        note[2, 2:3, :] = near(-1.0)
        note[2, 3:4, :] = (
            jnp.exp(-rate) * jnp.sum(cross, axis=0, keepdims=True) + lag_ref[...]
        )

    def begin(d):
        down = d == 1
        mine = iota((groups, width), 1) // modes == iota((groups, width), 0)
        response = fine_dot(jnp.where(mine, res, 0.0), powers(rate, 0.0, down), 1, 1)
        high, low = split(jnp.transpose(res * powers(rate, 1.0, down)))
        state = jnp.concatenate(states[d], axis=0)
        wide = state.astype(BF16).astype(F32)
        fine = pltpu.roll(state - wide, 2 * modes, 1)
        again = pltpu.roll(wide, 4 * modes, 1)
        own[d] = (response, high, low, wide, fine, again)

    def group(d, g):
        down = d == 1
        response, high, low, wide, fine, again = own[d]
        square = (BLOCK, BLOCK)
        keep = iota(square, 1) <= iota(square, 0) if down else iota(square, 1) >= iota(square, 0)
        line = jnp.broadcast_to(response[g : g + 1], (8, BLOCK))
        line = pltpu.roll(line, int(down), 1, stride=1, stride_axis=0)
        parts = [line] + [pltpu.roll(line, 8 * i, 1) for i in range(1, BLOCK // 8)]
        ts[d, g] = jnp.concatenate(parts, axis=0).astype(BF16) * mask(keep)
        rows = slice(g * modes, (g + 1) * modes)
        for turns, piece in ((0, high), (1, high), (2, low)):
            at = (g * modes + 2 * modes * turns) % width
            rs[d, g, at : at + modes, :] = piece[rows]
        if g % 2 == 0:
            p = g // 2
            quarter = iota((count * members, width), 1) // (2 * modes)
            lefts[d] = jnp.where(
                quarter == p, wide, jnp.where(quarter == (p + 1) % 4, fine, again)
            ).astype(BF16)
        source = (x_ref, h_ref)[d]
        both = jnp.concatenate([source[:, g * BLOCK : (g + 1) * BLOCK], lefts[d]], axis=1)
        out = dot(both, jnp.concatenate([ts[d, g], rs[d, g]], axis=0))
        for n in range(count):
            turn[d, n, g * members : (g + 1) * members, :] = out[n * members : (n + 1) * members]

    steps = [prepare]
    for d in range(2):
        steps.append(functools.partial(begin, d))
        steps.extend(functools.partial(group, d, g) for g in range(groups))
    return steps


def turn_steps(length, turn, lo, gg):
    def step(n):
        rows = slice(n * BLOCK, (n + 1) * BLOCK)
        lo[rows, :] = jnp.transpose(turn[0, n])
        gg[rows, :] = jnp.transpose(turn[1, n])

    return [functools.partial(step, n) for n in reversed(range(length // BLOCK))]


def output_steps(
    sizes, q_ref, k_ref, v_ref, c_ref, prior_ref, after_ref, taps_ref, short_refs,
    mixed_ref, gq_ref, gk_ref, gv_ref, terms_ref, us, es, note, lo, gg,
):
    members, modes, taps, ctx = sizes
    length = q_ref.shape[0]
    count = length // BLOCK
    span = taps - 1
    streams = (q_ref, k_ref, v_ref)
    part = PART
    ones = jnp.ones((8, BLOCK), BF16)
    sums = [jnp.zeros((8, LANES), F32) for _ in range(3 * taps)]

    def prepare():
        head = after_ref[...].astype(F32)
        rest = jnp.zeros((PAD - span, LANES), F32)
        ends = []
        for i in range(3):
            if i in short_refs:
                us[i, PAD + length - span : PAD + length, :] = streams[i][
                    length - span :, :
                ].astype(F32)
            else:
                us[i, PAD - span : PAD, :] = prior_ref[i * span : (i + 1) * span, :].astype(F32)
                us[i, PAD : PAD + length, :] = streams[i][...].astype(F32)
            us[i, PAD + length : 2 * PAD + length, :] = jnp.concatenate(
                [head[i * span : (i + 1) * span], rest], axis=0
            )
            ends.append(short(taps_ref, i, windows(us, i, length, PAD, taps)))
        query, key, value = ends
        cot = jnp.concatenate([head[3 * span : 4 * span], rest], axis=0)
        line = jnp.zeros((1, LANES), F32)
        second = iota((PAD, LANES), 0) == 1
        gated = (key * value).astype(BF16).astype(F32)
        grad_long = (cot * query).astype(BF16).astype(F32)
        gated_prev = jnp.where(second, jnp.concatenate([line, gated[:-1]], axis=0), 0.0)
        grad_prev = jnp.where(second, jnp.concatenate([line, grad_long[:-1]], axis=0), 0.0)
        out = note[0] + note[2, 0:1, :] * gated + note[2, 1:2, :] * gated_prev
        back = note[1] - note[2, 2:3, :] * grad_prev
        for i, edge in enumerate((cot * out, back * value, back * key)):
            es[i, length : length + PAD, :] = edge

    def tap(i, j):
        return jnp.broadcast_to(taps_ref[i, j : j + 1, :], (16, LANES)).astype(BF16)

    def scale(value, row):
        return (value.reshape(value.shape[0] // 16, 16, LANES) * row[None]).reshape(value.shape)

    tap_rows = [[tap(i, j) for j in range(taps)] for i in range(3)]

    def block(n):
        products = [[] for _ in range(3 * taps)]
        for start in reversed(range(n * BLOCK, (n + 1) * BLOCK, part)):
            rows = slice(start, start + part)
            long_out, grad_gated = lo[rows, :], gg[rows, :]
            key, value = [short_refs[i][rows, :].astype(F32) for i in (1, 2)]
            mixed_ref[rows, :] = short_refs[0][rows, :] * long_out.astype(BF16)
            edges = (c_ref[rows, :].astype(F32) * long_out, grad_gated * value, grad_gated * key)
            for i, (edge, target) in enumerate(zip(edges, (gq_ref, gk_ref, gv_ref))):
                es[i, rows, :] = edge
                stream = streams[i][rows, :]
                total = None
                for j in range(taps):
                    later = (es[i, start + j : start + j + part, :] if j else edge).astype(BF16)
                    products[i * taps + j].insert(0, later * stream)
                    term = scale(later, tap_rows[i][j])
                    total = term if total is None else total + term
                target[rows, :] = total
        for a in range(0, 3 * taps, 2):
            wide = [jnp.concatenate(p, axis=0) for p in products[a : a + 2]]
            added = dot(ones, jnp.concatenate(wide, axis=1))
            for at in range(len(wide)):
                sums[a + at] = sums[a + at] + added[:, at * LANES : (at + 1) * LANES]

    def end():
        high, low = split(note[2, 3:4, :])
        lines = [s[0:1] for s in sums] + [high.astype(F32), low.astype(F32)]
        lines.append(jnp.zeros((16 - len(lines), LANES), F32))
        terms = jnp.concatenate(lines, axis=0).astype(BF16)
        for j in range(ctx):
            terms_ref[j] = terms

    blocks = [functools.partial(block, n) for n in reversed(range(count))]
    return prepare, blocks, end


def finish_kernel(sizes, *refs):
    members = sizes[0]
    me_ref, q_ref, k_ref, v_ref, c_ref, prior_ref, after_ref, taps_ref, rate_ref, res_ref = refs[:10]
    lag_ref, x_ref, h_ref, ef_ref, eb_ref, recv_ref = refs[10:16]
    kept, rest = refs[16 : 16 + len(KEPT)], refs[16 + len(KEPT) :]
    mixed_ref, gq_ref, gk_ref, gv_ref, terms_ref, us, es, ts, rs, turn, note, lo, gg = rest
    length = q_ref.shape[0]
    groups = LANES // members
    rows = x_ref.shape[0] // TILES
    step, last = pl.program_id(0), pl.num_programs(0) - 1

    def convolve(t):
        part, own = pl.ds(t * rows, rows), slice(t * groups, (t + 1) * groups)
        return conv_steps(
            sizes, length, me_ref[0], rate_ref[own, :], res_ref[own, :], lag_ref.at[t],
            *[r.at[part, :] for r in (x_ref, h_ref, ef_ref, eb_ref)],
            recv_ref.at[:, pl.ds(t * members, members), :],
            ts.at[t], rs.at[t], turn.at[t], note.at[1, t],
        )

    def output(t):
        lanes = pl.ds(t * LANES, LANES)
        return output_steps(
            sizes, *[r.at[:, lanes] for r in (q_ref, k_ref, v_ref, c_ref, prior_ref, after_ref)],
            taps_ref.at[:, :, lanes], {i: r.at[:, lanes] for i, r in zip(KEPT, kept)},
            *[r.at[:, lanes] for r in (mixed_ref, gq_ref, gk_ref, gv_ref)],
            terms_ref.at[:, :, lanes], us.at[t], es.at[t], note.at[0, t], lo.at[t], gg.at[t],
        )

    def settle(t):
        note[0, t] = note[1, t]

    @pl.when(step == 0)
    def _():
        rs[...] = jnp.zeros_like(rs)
        for t in range(TILES):
            for run in convolve(t) + turn_steps(length, turn.at[t], lo.at[t], gg.at[t]):
                run()
            settle(t)

    @pl.when((step > 0) & (step < last))
    def _():
        for t in range(TILES):
            prepare, blocks, end = output(t)
            work = convolve(t)
            turns = turn_steps(length, turn.at[t], lo.at[t], gg.at[t])
            early = (len(blocks) + 1) // 2
            share = -(-len(work) // early)
            prepare()
            ready = 0
            for k, block in enumerate(blocks):
                for run in work[k * share : (k + 1) * share]:
                    run()
                block()
                if (k + 1) * share >= len(work):
                    while ready <= k and ready < (k + 1 - early) * 2 + 2:
                        turns[ready]()
                        ready += 1
            for run in turns[ready:]:
                run()
            end()
            settle(t)

    @pl.when(step == last)
    def _():
        for t in range(TILES):
            prepare, blocks, end = output(t)
            for run in [prepare] + blocks + [end]:
                run()


def local(q, k, v, c, short_taps, residues, rates):
    length, wide = q.shape
    taps = short_taps.shape[1]
    span = taps - 1
    groups, modes = residues.shape
    members = wide // groups
    ctx = lax.axis_size("ctx")
    tiles = wide // LANES
    per = LANES // members
    width = per * modes
    rows = length // BLOCK * members
    lanes = per * BLOCK
    sizes = (members, modes, taps, ctx)
    me = lax.axis_index("ctx").astype(jnp.int32).reshape(1)
    prior = lax.ppermute(
        jnp.concatenate([q[length - span :], k[length - span :], v[length - span :]], axis=0),
        "ctx", [(i, i + 1) for i in range(ctx - 1)],
    )
    after = lax.ppermute(
        jnp.concatenate([q[:span], k[:span], v[:span], c[:span]], axis=0),
        "ctx", [(i + 1, i) for i in range(ctx - 1)],
    )

    smem = pl.BlockSpec(memory_space=pltpu.SMEM)
    stream = pl.BlockSpec((length, TILES * LANES), lambda i: (0, i))
    tap_spec = pl.BlockSpec((3, taps, TILES * LANES), lambda i: (0, 0, i))
    group_spec = pl.BlockSpec((TILES * per, modes), lambda i: (i, 0))
    row = pl.BlockSpec((TILES, 1, width), lambda i: (i, 0, 0))
    turned = pl.BlockSpec((TILES * rows, lanes), lambda i: (i, 0))
    ends = pl.BlockSpec((TILES * rows, width), lambda i: (i, 0))
    swap = pl.BlockSpec((ctx, TILES * members, width), lambda i: (0, i, 0))

    def strip(n):
        return pl.BlockSpec((n, TILES * LANES), lambda i: (0, i))

    turned_shape = jax.ShapeDtypeStruct((tiles * rows, lanes), BF16)
    ends_shape = jax.ShapeDtypeStruct((tiles * rows, width), F32)
    big = jax.ShapeDtypeStruct((length, wide), BF16)
    x, h, ef, eb, send, *kept = pl.pallas_call(
        functools.partial(states_kernel, sizes),
        grid=(tiles // TILES,),
        in_specs=[smem, stream, stream, stream, stream, strip(3 * span), tap_spec, group_spec],
        out_specs=[turned, turned, ends, ends, swap] + [stream] * len(KEPT),
        out_shape=[
            turned_shape, turned_shape, ends_shape, ends_shape,
            jax.ShapeDtypeStruct((ctx, tiles * members, width), F32),
        ] + [big] * len(KEPT),
        scratch_shapes=[
            pltpu.VMEM((TILES, 3, PAD + length, LANES), F32),
            pltpu.VMEM((TILES, length, LANES), BF16),
            pltpu.VMEM((TILES, length, LANES), BF16),
            pltpu.VMEM((TILES, lanes, 2 * width), BF16),
            pltpu.VMEM((TILES, lanes, 2 * width), BF16),
        ],
        cost_estimate=pl.CostEstimate(flops=4 * 10**9, bytes_accessed=34 * 10**6, transcendentals=0),
        name="states",
    )(me, q, k, v, c, prior, short_taps, rates)
    recv = lax.all_to_all(send, "ctx", split_axis=0, concat_axis=0, tiled=True)
    lag = pl.pallas_call(
        functools.partial(pairs_kernel, sizes),
        grid=(tiles // TILES,),
        in_specs=[turned, turned, group_spec],
        out_specs=row,
        out_shape=jax.ShapeDtypeStruct((tiles, 1, width), F32),
        cost_estimate=pl.CostEstimate(flops=4 * 10**9, bytes_accessed=17 * 10**6, transcendentals=0),
        name="pairs",
    )(x, h, rates)
    steps = tiles // TILES

    def late(spec):
        return pl.BlockSpec(spec.block_shape, lambda i: spec.index_map(jnp.maximum(i - 1, 0)))

    def soon(spec):
        return pl.BlockSpec(spec.block_shape, lambda i: spec.index_map(jnp.minimum(i, steps - 1)))

    lines = late(stream)
    mixed, gq, gk, gv, terms = pl.pallas_call(
        functools.partial(finish_kernel, sizes),
        grid=(steps + 1,),
        in_specs=[
            smem, lines, lines, lines, lines, late(strip(3 * span)), late(strip(4 * span)),
            late(tap_spec), soon(group_spec), soon(group_spec), soon(row), soon(turned),
            soon(turned), soon(ends), soon(ends), soon(swap),
        ] + [lines] * len(KEPT),
        out_specs=[
            lines, lines, lines, lines,
            late(pl.BlockSpec((ctx, 16, TILES * LANES), lambda i: (0, 0, i))),
        ],
        out_shape=[big, big, big, big, jax.ShapeDtypeStruct((ctx, 16, wide), BF16)],
        scratch_shapes=[
            pltpu.VMEM((TILES, 3, 2 * PAD + length, LANES), F32),
            pltpu.VMEM((TILES, 3, PAD + length, LANES), F32),
            pltpu.VMEM((TILES, 2, per, BLOCK, BLOCK), BF16),
            pltpu.VMEM((TILES, 2, per, width, BLOCK), BF16),
            pltpu.VMEM((TILES, 2, length // BLOCK, LANES, BLOCK), F32),
            pltpu.VMEM((2, TILES, 3, PAD, LANES), F32),
            pltpu.VMEM((TILES, length, LANES), F32),
            pltpu.VMEM((TILES, length, LANES), F32),
        ],
        cost_estimate=pl.CostEstimate(flops=8 * 10**9, bytes_accessed=50 * 10**6, transcendentals=0),
        name="finish",
    )(me, q, k, v, c, prior, after, short_taps, rates, residues, lag, x, h, ef, eb, recv, *kept)
    total = jnp.sum(
        lax.all_to_all(terms, "ctx", split_axis=0, concat_axis=0, tiled=True).astype(F32), axis=0
    )
    count = 3 * taps
    grad_taps = total[:count].reshape(3, taps, wide)
    grad_res = (total[count] + total[count + 1]).reshape(groups, modes)
    return mixed, gq, gk, gv, grad_taps, grad_res


def solution(mesh):
    stream = P("ctx", "tp")
    return jax.shard_map(
        local,
        mesh=mesh,
        in_specs=(stream, stream, stream, stream, P(None, None, "tp"), P("tp", None), P("tp", None)),
        out_specs=(stream, stream, stream, stream, P(None, None, "tp"), P("tp", None)),
        check_vma=False,
    )
```

time: 124 us -> 106 us (0.85)
  Pallas kernels: 86 us -> 71.4 us
  local copies, waits for them, and re-layouts: 12.5 us -> 6.83 us
  blocking collectives: 15.3 us -> 13.1 us
  waiting for transfers between devices: 0.01 us -> 2.1 us
  starting transfers between devices: 8.7 us -> 10.3 us
    pallas_call x3, Pallas kernels: 86 us -> 71.4 us  [the longest x1 40 us: local(): pl.pallas_call(functools.partial(finish_kernel, sizes), grid=(steps + 1,)...]
    reshape x6 -> x0, local copies, waits for them, and re-layouts: 6.8 us -> none  [the longest x1 1.58 us: local(): tap_rows = short_taps.reshape(3 * taps, wide)]
    all_to_all x1, blocking collectives: 15.3 us -> 13.1 us  [local(): lax.all_to_all(terms, 'ctx', split_axis=0, concat_axis=0, tiled=True)]
    all_to_all x1, waiting for transfers between devices: 0.01 us -> 2.09 us  [local(): recv = lax.all_to_all(send, 'ctx', split_axis=0, concat_axis=0, tiled=True)]
    all_to_all x1, starting transfers between devices: 5.01 us -> 6.6 us  [local(): recv = lax.all_to_all(send, 'ctx', split_axis=0, concat_axis=0, tiled=True)]
    unnamed x13 -> x11, local copies, waits for them, and re-layouts: 3.16 us -> 4.44 us
  transfers between devices with their start and end apart: 3 -> 3, of which waited for: 0 -> 1; matrix products, arithmetic and copies ran while one was open for 6% -> 2% of each run, Pallas kernels for 26% -> 11%
where the time goes in v2:
time: 106 us; the launch traced here: 105 us
  Pallas kernels  71.4 us (67%)
  blocking collectives  13.1 us (12%)
  starting transfers between devices  10.3 us (10%)
  local copies, waits for them, and re-layouts  6.83 us (6%)
  waiting for transfers between devices  2.1 us (2%)
    pallas_call x1, Pallas kernels, local(): pl.pallas_call(functools.partial(finish_kernel, sizes), grid=(steps + 1,)...  40 us
    pallas_call x1, Pallas kernels, local(): pl.pallas_call(functools.partial(states_kernel, sizes), grid=(tiles // TI...  20.2 us
    all_to_all x1, blocking collectives, local(): lax.all_to_all(terms, 'ctx', split_axis=0, concat_axis=0, tiled=True)  13.1 us
    pallas_call x1, Pallas kernels, local(): pl.pallas_call(functools.partial(pairs_kernel, sizes), grid=(tiles // TIL...  11.2 us
    all_to_all x1, starting transfers between devices, local(): recv = lax.all_to_all(send, 'ctx', split_axis=0, concat_axis=0, tiled=True)  6.6 us
    unnamed x11, local copies, waits for them, and re-layouts  4.44 us
    ppermute x1, starting transfers between devices, local(): lax.ppermute(jnp.concatenate([q[length - span:], k[length - span:], v[len...  2.4 us
  transfers between devices with their start and end apart: 3, of which 1 were waited for; matrix products, arithmetic and copies ran while one was open for 2% of the time, Pallas kernels for 11%

profile of v2, /device:TPU:0, one launch (start us, length us, event | category | flops | bytes accessed | tf_op | source)
XLA Modules:
  0.0 104.6 jit_solution(16345440153237235065)
XLA Ops:
  0.6 0.8 fusion.3
  1.4 0.8 fusion.1
  2.3 2.4 %collective-permute-start = (bf16[6,2048]{1,0:T(8,128)(2,1)S(1)}, bf16[6,2048]{1,0:T(8,128)(2,1)S(1)}, u32[]{:S(2)}, u32[]{:S(2)}) collective-permute-start(bf16[6,2048]{1,0:T(8,128)(2,1)S(1)} %pad_maximum_fusion), channel_id=1, source_target_pairs={{0,4},{4,8},{8,12},{12,16},{16,20},{20,24},{24,28},{1,5},{5,9},{9,... | collective-permute-start | bytes 73736 | tf_op jit(solution)/shard_map/ppermute | solution.py:485
  4.7 1.4 %copy.19.refs_7_.rate_ref.refs_8_ = f32[128,16]{1,0:T(8,128)} copy(f32[128,16]{0,1:T(8,128)} %param.13) | data formatting | bytes 16384 | tf_op args[6]
  6.2 0.0 collective-permute-done.refs_5_
  6.2 0.0 copy-start.1
  6.2 0.6 copy-done.1
  6.8 0.0 slice-start
  6.8 0.0 copy-start.3
  6.8 20.2 %states.1 = (bf16[2048,1024]{1,0:T(8,128)(2,1)}, bf16[2048,1024]{1,0:T(8,128)(2,1)}, f32[2048,128]{1,0:T(8,128)}, f32[2048,128]{1,0:T(8,128)}, f32[8,256,128]{2,...) custom-call(s32[1]{0:T(128)} %bitcast.refs_0_, ...), custom_call_target="tpu_custom_call" | custom-call | flops 4000000000 | bytes 34000000 | tf_op jit(solution)/shard_map/states/pallas_call | solution.py:509
  27.0 6.6 %all-to-all-start = ((f32[8,256,128]{2,1,0:T(8,128)}), f32[8,256,128]{2,1,0:T(8,128)S(1)}, u32[]{:S(2)}, u32[]{:S(2)}) async-start(f32[8,256,128]{2,1,0:T(8,128)} %get-tuple-element.23), calls=%async_computation | async-start | bytes 2097152 | tf_op jit(solution)/shard_map/all_to_all | solution.py:528
  33.6 0.0 slice-done
  33.7 1.3 %collective-permute-start.1 = (bf16[8,2048]{1,0:T(8,128)(2,1)S(1)}, bf16[8,2048]{1,0:T(8,128)(2,1)S(1)}, u32[]{:S(2)}, u32[]{:S(2)}) collective-permute-start(bf16[8,2048]{1,0:T(8,128)(2,1)S(1)} %pad_maximum_fusion.1), channel_id=1, source_target_pairs={{4,0},{8,4},{12,8},{16,12},{20,16},{24,20},{28,24},{5,1},{9,5},{13... | collective-permute-start | bytes 98312 | tf_op jit(solution)/shard_map/ppermute | solution.py:489
  35.0 0.0 copy-done.3
  35.0 0.7 copy.20.refs_9_
  35.7 11.2 %pairs.1.refs_10_ = f32[16,1,128]{2,1,0:T(1,128)} custom-call(bf16[2048,1024]{1,0:T(8,128)(2,1)} %get-tuple-element.19.x_ref.refs_11_, bf16[2048,1024]{1,0:T(8,128)(2,1)} %get-tuple-element.20.h_ref.refs_12_, f32[128,16]{1,0:T(8,128)} %copy.19.refs_7_.rate_ref.refs_8_), custom_call_target="tpu_custom_call" | custom-call | flops 4000000000 | bytes 17000000 | tf_op jit(solution)/shard_map/pairs/pallas_call | solution.py:529
  46.9 0.0 collective-permute-done.1.refs_6_
  46.9 0.0 copy-start.2
  46.9 2.1 %all-to-all-done.refs_15_ = f32[8,256,128]{2,1,0:T(8,128)S(1)} async-done(((f32[8,256,128]{2,1,0:T(8,128)}), f32[8,256,128]{2,1,0:T(8,128)S(1)}, u32[]{:S(2)}, u32[]{:S(2)}) %all-to-all-start) | async-done | bytes 1048608 | tf_op jit(solution)/shard_map/all_to_all | solution.py:528
  49.0 0.0 copy-start
  49.0 0.0 copy-done.2
  49.0 1.0 copy-done
  50.0 40.0 %finish.1 = (bf16[1024,2048]{1,0:T(8,128)(2,1)}, bf16[1024,2048]{1,0:T(8,128)(2,1)}, bf16[1024,2048]{1,0:T(8,128)(2,1)}, bf16[1024,2048]{1,0:T(8,128)(2,1)}, bf16[8,16,2048]{2,1,0:T(8,128)(2,1)}) custom-call(s32[1]{0:T(128)} %bitcast.refs_0_, bf16[1024,2048]{1,0:T(8,128)(2,1)} %refs_1_.3, bf16[1024,2048]{1,0:T(8,128)(2,1)} %refs_2_.3, ...), custom_call_target="tpu_custom_call" | custom-call | flops 8000000000 | bytes 50000000 | tf_op jit(solution)/shard_map/finish/pallas_call | solution.py:547
  90.0 13.1 %all_to_all.10 = bf16[8,16,2048]{2,1,0:T(8,128)(2,1)S(1)} all-to-all(bf16[8,16,2048]{2,1,0:T(8,128)(2,1)} %get-tuple-element.31), channel_id=1, replica_groups=mesh['ctx'=8,'tp'=4] {'ctx'}, dimensions={0} | all-to-all | bytes 1048576 | tf_op jit(solution)/shard_map/all_to_all | solution.py:574
  103.1 0.1 convert_reduce_fusion
  103.2 0.1 add.8
  103.3 0.7 copy.21
  104.0 0.7 reshape.23
  (3 shorter events, 0.1 us)
Async XLA Ops:
  2.3 3.8 %collective-permute-start = (bf16[6,2048]{1,0:T(8,128)(2,1)S(1)}, bf16[6,2048]{1,0:T(8,128)(2,1)S(1)}, u32[]{:S(2)}, u32[]{:S(2)}) collective-permute-start(bf16[6,2048]{1,0:T(8,128)(2,1)S(1)} %pad_maximum_fusion), channel_id=1, source_target_pairs={{0,4},{4,8},{8,12},{12,16},{16,20},{20,24},{24,28},{1,5},{5,9},{9,... | collective-permute-start | bytes 73736 | tf_op jit(solution)/shard_map/ppermute | solution.py:485
  6.2 0.6 copy-start.1
  6.8 26.8 %slice-start = ((bf16[1024,2048]{1,0:T(8,128)(2,1)}), bf16[2,2048]{1,0:T(2,128)(2,1)S(1)}, s32[]{:S(2)}) async-start(bf16[1024,2048]{1,0:T(8,128)(2,1)} %refs_4_.3), calls=%async_computation.2 | async-start | bytes 16384 | tf_op jit(solution)/shard_map/slice | solution.py:490
  6.8 28.2 %copy-start.3 = (f32[128,16]{0,1:T(8,128)S(1)}, f32[128,16]{0,1:T(8,128)}, u32[]{:S(2)}) copy-start(f32[128,16]{0,1:T(8,128)} %param.12) | copy-start | bytes 24580
  27.0 22.0 %all-to-all-start = ((f32[8,256,128]{2,1,0:T(8,128)}), f32[8,256,128]{2,1,0:T(8,128)S(1)}, u32[]{:S(2)}, u32[]{:S(2)}) async-start(f32[8,256,128]{2,1,0:T(8,128)} %get-tuple-element.23), calls=%async_computation | async-start | bytes 2097152 | tf_op jit(solution)/shard_map/all_to_all | solution.py:528
  33.7 13.2 %collective-permute-start.1 = (bf16[8,2048]{1,0:T(8,128)(2,1)S(1)}, bf16[8,2048]{1,0:T(8,128)(2,1)S(1)}, u32[]{:S(2)}, u32[]{:S(2)}) collective-permute-start(bf16[8,2048]{1,0:T(8,128)(2,1)S(1)} %pad_maximum_fusion.1), channel_id=1, source_target_pairs={{4,0},{8,4},{12,8},{16,12},{20,16},{24,20},{28,24},{5,1},{9,5},{13... | collective-permute-start | bytes 98312 | tf_op jit(solution)/shard_map/ppermute | solution.py:489
  46.9 2.1 %copy-start.2 = (bf16[8,2048]{1,0:T(8,128)(2,1)}, bf16[8,2048]{1,0:T(8,128)(2,1)S(1)}, u32[]{:S(2)}) copy-start(bf16[8,2048]{1,0:T(8,128)(2,1)S(1)} %collective-permute-done.1.refs_6_) | copy-start | bytes 98308
  49.0 1.0 copy-start

commit v3 on v2

--- a/solution.py
+++ b/solution.py
@@ -443,7 +443,7 @@
             prepare, blocks, end = output(t)
             work = convolve(t)
             turns = turn_steps(length, turn.at[t], lo.at[t], gg.at[t])
-            early = (len(blocks) + 1) // 2
+            early = len(blocks)
             share = -(-len(work) // early)
             prepare()
             ready = 0

time: 106 us -> 105 us (level)
  no operation moved by 1% of the time
where the time goes in v3:
time: 105 us; the launch traced here: 104 us
  Pallas kernels  70.4 us (67%)
  blocking collectives  13.1 us (12%)
  starting transfers between devices  10.3 us (10%)
  local copies, waits for them, and re-layouts  6.83 us (7%)
  waiting for transfers between devices  2.1 us (2%)
    pallas_call x1, Pallas kernels, local(): pl.pallas_call(functools.partial(finish_kernel, sizes), grid=(steps + 1,)...  39 us
    pallas_call x1, Pallas kernels, local(): pl.pallas_call(functools.partial(states_kernel, sizes), grid=(tiles // TI...  20.2 us
    all_to_all x1, blocking collectives, local(): lax.all_to_all(terms, 'ctx', split_axis=0, concat_axis=0, tiled=True)  13.1 us
    pallas_call x1, Pallas kernels, local(): pl.pallas_call(functools.partial(pairs_kernel, sizes), grid=(tiles // TIL...  11.2 us
    all_to_all x1, starting transfers between devices, local(): recv = lax.all_to_all(send, 'ctx', split_axis=0, concat_axis=0, tiled=True)  6.6 us
    unnamed x11, local copies, waits for them, and re-layouts  4.44 us
    ppermute x1, starting transfers between devices, local(): lax.ppermute(jnp.concatenate([q[length - span:], k[length - span:], v[len...  2.4 us
  transfers between devices with their start and end apart: 3, of which 1 were waited for; matrix products, arithmetic and copies ran while one was open for 2% of the time, Pallas kernels for 11%

profile of v3, /device:TPU:0, one launch (start us, length us, event | category | flops | bytes accessed | tf_op | source)
XLA Modules:
  0.0 103.7 jit_solution(11367854774947567473)
XLA Ops:
  0.6 0.8 fusion.3
  1.4 0.8 fusion.1
  2.3 2.4 %collective-permute-start = (bf16[6,2048]{1,0:T(8,128)(2,1)S(1)}, bf16[6,2048]{1,0:T(8,128)(2,1)S(1)}, u32[]{:S(2)}, u32[]{:S(2)}) collective-permute-start(bf16[6,2048]{1,0:T(8,128)(2,1)S(1)} %pad_maximum_fusion), channel_id=1, source_target_pairs={{0,4},{4,8},{8,12},{12,16},{16,20},{20,24},{24,28},{1,5},{5,9},{9,... | collective-permute-start | bytes 73736 | tf_op jit(solution)/shard_map/ppermute | solution.py:485
  4.7 1.4 %copy.19.refs_7_.rate_ref.refs_8_ = f32[128,16]{1,0:T(8,128)} copy(f32[128,16]{0,1:T(8,128)} %param.13) | data formatting | bytes 16384 | tf_op args[6]
  6.2 0.0 collective-permute-done.refs_5_
  6.2 0.0 copy-start.1
  6.2 0.6 copy-done.1
  6.8 0.0 slice-start
  6.8 0.0 copy-start.3
  6.8 20.2 %states.1 = (bf16[2048,1024]{1,0:T(8,128)(2,1)}, bf16[2048,1024]{1,0:T(8,128)(2,1)}, f32[2048,128]{1,0:T(8,128)}, f32[2048,128]{1,0:T(8,128)}, f32[8,256,128]{2,...) custom-call(s32[1]{0:T(128)} %bitcast.refs_0_, ...), custom_call_target="tpu_custom_call" | custom-call | flops 4000000000 | bytes 34000000 | tf_op jit(solution)/shard_map/states/pallas_call | solution.py:509
  27.0 6.6 %all-to-all-start = ((f32[8,256,128]{2,1,0:T(8,128)}), f32[8,256,128]{2,1,0:T(8,128)S(1)}, u32[]{:S(2)}, u32[]{:S(2)}) async-start(f32[8,256,128]{2,1,0:T(8,128)} %get-tuple-element.23), calls=%async_computation | async-start | bytes 2097152 | tf_op jit(solution)/shard_map/all_to_all | solution.py:528
  33.6 0.0 slice-done
  33.7 1.3 %collective-permute-start.1 = (bf16[8,2048]{1,0:T(8,128)(2,1)S(1)}, bf16[8,2048]{1,0:T(8,128)(2,1)S(1)}, u32[]{:S(2)}, u32[]{:S(2)}) collective-permute-start(bf16[8,2048]{1,0:T(8,128)(2,1)S(1)} %pad_maximum_fusion.1), channel_id=1, source_target_pairs={{4,0},{8,4},{12,8},{16,12},{20,16},{24,20},{28,24},{5,1},{9,5},{13... | collective-permute-start | bytes 98312 | tf_op jit(solution)/shard_map/ppermute | solution.py:489
  35.0 0.0 copy-done.3
  35.0 0.7 copy.20.refs_9_
  35.7 11.2 %pairs.1.refs_10_ = f32[16,1,128]{2,1,0:T(1,128)} custom-call(bf16[2048,1024]{1,0:T(8,128)(2,1)} %get-tuple-element.19.x_ref.refs_11_, bf16[2048,1024]{1,0:T(8,128)(2,1)} %get-tuple-element.20.h_ref.refs_12_, f32[128,16]{1,0:T(8,128)} %copy.19.refs_7_.rate_ref.refs_8_), custom_call_target="tpu_custom_call" | custom-call | flops 4000000000 | bytes 17000000 | tf_op jit(solution)/shard_map/pairs/pallas_call | solution.py:529
  46.9 0.0 collective-permute-done.1.refs_6_
  46.9 0.0 copy-start.2
  46.9 2.1 %all-to-all-done.refs_15_ = f32[8,256,128]{2,1,0:T(8,128)S(1)} async-done(((f32[8,256,128]{2,1,0:T(8,128)}), f32[8,256,128]{2,1,0:T(8,128)S(1)}, u32[]{:S(2)}, u32[]{:S(2)}) %all-to-all-start) | async-done | bytes 1048608 | tf_op jit(solution)/shard_map/all_to_all | solution.py:528
  49.0 0.0 copy-start
  49.0 0.0 copy-done.2
  49.0 1.0 copy-done
  50.0 39.0 %finish.1 = (bf16[1024,2048]{1,0:T(8,128)(2,1)}, bf16[1024,2048]{1,0:T(8,128)(2,1)}, bf16[1024,2048]{1,0:T(8,128)(2,1)}, bf16[1024,2048]{1,0:T(8,128)(2,1)}, bf16[8,16,2048]{2,1,0:T(8,128)(2,1)}) custom-call(s32[1]{0:T(128)} %bitcast.refs_0_, bf16[1024,2048]{1,0:T(8,128)(2,1)} %refs_1_.3, bf16[1024,2048]{1,0:T(8,128)(2,1)} %refs_2_.3, ...), custom_call_target="tpu_custom_call" | custom-call | flops 8000000000 | bytes 50000000 | tf_op jit(solution)/shard_map/finish/pallas_call | solution.py:547
  89.0 13.1 %all_to_all.10 = bf16[8,16,2048]{2,1,0:T(8,128)(2,1)S(1)} all-to-all(bf16[8,16,2048]{2,1,0:T(8,128)(2,1)} %get-tuple-element.31), channel_id=1, replica_groups=mesh['ctx'=8,'tp'=4] {'ctx'}, dimensions={0} | all-to-all | bytes 1048576 | tf_op jit(solution)/shard_map/all_to_all | solution.py:574
  102.1 0.1 convert_reduce_fusion
  102.2 0.1 add.8
  102.3 0.7 copy.21
  103.0 0.7 reshape.23
  (3 shorter events, 0.1 us)
Async XLA Ops:
  2.3 3.8 %collective-permute-start = (bf16[6,2048]{1,0:T(8,128)(2,1)S(1)}, bf16[6,2048]{1,0:T(8,128)(2,1)S(1)}, u32[]{:S(2)}, u32[]{:S(2)}) collective-permute-start(bf16[6,2048]{1,0:T(8,128)(2,1)S(1)} %pad_maximum_fusion), channel_id=1, source_target_pairs={{0,4},{4,8},{8,12},{12,16},{16,20},{20,24},{24,28},{1,5},{5,9},{9,... | collective-permute-start | bytes 73736 | tf_op jit(solution)/shard_map/ppermute | solution.py:485
  6.2 0.6 copy-start.1
  6.8 26.8 %slice-start = ((bf16[1024,2048]{1,0:T(8,128)(2,1)}), bf16[2,2048]{1,0:T(2,128)(2,1)S(1)}, s32[]{:S(2)}) async-start(bf16[1024,2048]{1,0:T(8,128)(2,1)} %refs_4_.3), calls=%async_computation.2 | async-start | bytes 16384 | tf_op jit(solution)/shard_map/slice | solution.py:490
  6.8 28.2 %copy-start.3 = (f32[128,16]{0,1:T(8,128)S(1)}, f32[128,16]{0,1:T(8,128)}, u32[]{:S(2)}) copy-start(f32[128,16]{0,1:T(8,128)} %param.12) | copy-start | bytes 24580
  27.0 22.0 %all-to-all-start = ((f32[8,256,128]{2,1,0:T(8,128)}), f32[8,256,128]{2,1,0:T(8,128)S(1)}, u32[]{:S(2)}, u32[]{:S(2)}) async-start(f32[8,256,128]{2,1,0:T(8,128)} %get-tuple-element.23), calls=%async_computation | async-start | bytes 2097152 | tf_op jit(solution)/shard_map/all_to_all | solution.py:528
  33.7 13.2 %collective-permute-start.1 = (bf16[8,2048]{1,0:T(8,128)(2,1)S(1)}, bf16[8,2048]{1,0:T(8,128)(2,1)S(1)}, u32[]{:S(2)}, u32[]{:S(2)}) collective-permute-start(bf16[8,2048]{1,0:T(8,128)(2,1)S(1)} %pad_maximum_fusion.1), channel_id=1, source_target_pairs={{4,0},{8,4},{12,8},{16,12},{20,16},{24,20},{28,24},{5,1},{9,5},{13... | collective-permute-start | bytes 98312 | tf_op jit(solution)/shard_map/ppermute | solution.py:489
  46.9 2.1 %copy-start.2 = (bf16[8,2048]{1,0:T(8,128)(2,1)}, bf16[8,2048]{1,0:T(8,128)(2,1)S(1)}, u32[]{:S(2)}) copy-start(bf16[8,2048]{1,0:T(8,128)(2,1)S(1)} %collective-permute-done.1.refs_6_) | copy-start | bytes 98308
  49.0 1.0 copy-start

commit v4 on v3

--- a/solution.py
+++ b/solution.py
@@ -11,6 +11,7 @@
 BLOCK = 128
 LANES = 128
 TILES = 2
+WIDE = 4
 PAD = 8
 PART = 64
 KEPT = (0, 1, 2)
@@ -111,10 +112,11 @@
             start = n * BLOCK + part * half
             rows = slice(start, start + half)
             shorts = [short(taps_ref, i, windows(us, i, start, half, taps)) for i in range(3)]
+            shorts = [value.astype(BF16) for value in shorts]
             for i, ref in short_refs.items():
-                ref[rows, :] = shorts[i].astype(BF16)
-            gs[rows, :] = (shorts[1] * shorts[2]).astype(BF16)
-            ls[rows, :] = (c_ref[rows, :].astype(F32) * shorts[0]).astype(BF16)
+                ref[rows, :] = shorts[i]
+            gs[rows, :] = shorts[1] * shorts[2]
+            ls[rows, :] = c_ref[rows, :] * shorts[0]
         if n % 2 == 0 and n + 1 < count:
             continue
         blocks = [n - 1, n] if n % 2 else [n]
@@ -156,8 +158,8 @@
     kept = refs[13 : 13 + len(KEPT)]
     us, gs, ls, af, ab = refs[13 + len(KEPT) :]
     groups = LANES // members
-    rows = x_ref.shape[0] // TILES
-    for t in range(TILES):
+    rows = x_ref.shape[0] // WIDE
+    for t in range(WIDE):
         lanes, part = pl.ds(t * LANES, LANES), pl.ds(t * rows, rows)
         states_tile(
             sizes, me_ref[0],
@@ -506,21 +508,27 @@
     turned_shape = jax.ShapeDtypeStruct((tiles * rows, lanes), BF16)
     ends_shape = jax.ShapeDtypeStruct((tiles * rows, width), F32)
     big = jax.ShapeDtypeStruct((length, wide), BF16)
+    def widen(spec):
+        shape, moved = list(spec.block_shape), spec.index_map(1)
+        at = [j for j, step in enumerate(moved) if not isinstance(step, int) or step == 1][0]
+        shape[at] = shape[at] // TILES * WIDE
+        return pl.BlockSpec(tuple(shape), spec.index_map)
+
     x, h, ef, eb, send, *kept = pl.pallas_call(
         functools.partial(states_kernel, sizes),
-        grid=(tiles // TILES,),
-        in_specs=[smem, stream, stream, stream, stream, strip(3 * span), tap_spec, group_spec],
-        out_specs=[turned, turned, ends, ends, swap] + [stream] * len(KEPT),
+        grid=(tiles // WIDE,),
+        in_specs=[smem] + [widen(p) for p in (stream,) * 4 + (strip(3 * span), tap_spec, group_spec)],
+        out_specs=[widen(p) for p in (turned, turned, ends, ends, swap) + (stream,) * len(KEPT)],
         out_shape=[
             turned_shape, turned_shape, ends_shape, ends_shape,
             jax.ShapeDtypeStruct((ctx, tiles * members, width), F32),
         ] + [big] * len(KEPT),
         scratch_shapes=[
-            pltpu.VMEM((TILES, 3, PAD + length, LANES), F32),
-            pltpu.VMEM((TILES, length, LANES), BF16),
-            pltpu.VMEM((TILES, length, LANES), BF16),
-            pltpu.VMEM((TILES, lanes, 2 * width), BF16),
-            pltpu.VMEM((TILES, lanes, 2 * width), BF16),
+            pltpu.VMEM((WIDE, 3, PAD + length, LANES), F32),
+            pltpu.VMEM((WIDE, length, LANES), BF16),
+            pltpu.VMEM((WIDE, length, LANES), BF16),
+            pltpu.VMEM((WIDE, lanes, 2 * width), BF16),
+            pltpu.VMEM((WIDE, lanes, 2 * width), BF16),
         ],
         cost_estimate=pl.CostEstimate(flops=4 * 10**9, bytes_accessed=34 * 10**6, transcendentals=0),
         name="states",

time: 105 us -> 104 us (level)
  no operation moved by 1% of the time
where the time goes in v4:
time: 104 us; the launch traced here: 103 us
  Pallas kernels  70 us (67%)
  blocking collectives  13.1 us (13%)
  starting transfers between devices  10.3 us (10%)
  local copies, waits for them, and re-layouts  6.83 us (7%)
  waiting for transfers between devices  2.1 us (2%)
    pallas_call x1, Pallas kernels, local(): pl.pallas_call(functools.partial(finish_kernel, sizes), grid=(steps + 1,)...  39 us
    pallas_call x1, Pallas kernels, local(): pl.pallas_call(functools.partial(states_kernel, sizes), grid=(tiles // WI...  19.8 us
    all_to_all x1, blocking collectives, local(): lax.all_to_all(terms, 'ctx', split_axis=0, concat_axis=0, tiled=True)  13.1 us
    pallas_call x1, Pallas kernels, local(): pl.pallas_call(functools.partial(pairs_kernel, sizes), grid=(tiles // TIL...  11.2 us
    all_to_all x1, starting transfers between devices, local(): recv = lax.all_to_all(send, 'ctx', split_axis=0, concat_axis=0, tiled=True)  6.6 us
    unnamed x11, local copies, waits for them, and re-layouts  4.44 us
    ppermute x1, starting transfers between devices, local(): lax.ppermute(jnp.concatenate([q[length - span:], k[length - span:], v[len...  2.4 us
    all_to_all x1, waiting for transfers between devices, local(): recv = lax.all_to_all(send, 'ctx', split_axis=0, concat_axis=0, tiled=True)  2.09 us
  transfers between devices with their start and end apart: 3, of which 1 were waited for; matrix products, arithmetic and copies ran while one was open for 2% of the time, Pallas kernels for 11%

profile of v4, /device:TPU:0, one launch (start us, length us, event | category | flops | bytes accessed | tf_op | source)
XLA Modules:
  0.0 103.2 jit_solution(13172013663971818171)
XLA Ops:
  0.6 0.8 fusion.3
  1.4 0.8 fusion.1
  2.3 2.4 %collective-permute-start = (bf16[6,2048]{1,0:T(8,128)(2,1)S(1)}, bf16[6,2048]{1,0:T(8,128)(2,1)S(1)}, u32[]{:S(2)}, u32[]{:S(2)}) collective-permute-start(bf16[6,2048]{1,0:T(8,128)(2,1)S(1)} %pad_maximum_fusion), channel_id=1, source_target_pairs={{0,4},{4,8},{8,12},{12,16},{16,20},{20,24},{24,28},{1,5},{5,9},{9,... | collective-permute-start | bytes 73736 | tf_op jit(solution)/shard_map/ppermute | solution.py:487
  4.7 1.4 %copy.19.refs_7_.rate_ref.refs_8_ = f32[128,16]{1,0:T(8,128)} copy(f32[128,16]{0,1:T(8,128)} %param.13) | data formatting | bytes 16384 | tf_op args[6]
  6.2 0.0 collective-permute-done.refs_5_
  6.2 0.0 copy-start.1
  6.2 0.6 copy-done.1
  6.8 0.0 slice-start
  6.8 0.0 copy-start.3
  6.8 19.8 %states.1 = (bf16[2048,1024]{1,0:T(8,128)(2,1)}, bf16[2048,1024]{1,0:T(8,128)(2,1)}, f32[2048,128]{1,0:T(8,128)}, f32[2048,128]{1,0:T(8,128)}, f32[8,256,128]{2,...) custom-call(s32[1]{0:T(128)} %bitcast.refs_0_, ...), custom_call_target="tpu_custom_call" | custom-call | flops 4000000000 | bytes 34000000 | tf_op jit(solution)/shard_map/states/pallas_call | solution.py:517
  26.6 6.6 %all-to-all-start = ((f32[8,256,128]{2,1,0:T(8,128)}), f32[8,256,128]{2,1,0:T(8,128)S(1)}, u32[]{:S(2)}, u32[]{:S(2)}) async-start(f32[8,256,128]{2,1,0:T(8,128)} %get-tuple-element.23), calls=%async_computation | async-start | bytes 2097152 | tf_op jit(solution)/shard_map/all_to_all | solution.py:536
  33.2 0.0 slice-done
  33.3 1.3 %collective-permute-start.1 = (bf16[8,2048]{1,0:T(8,128)(2,1)S(1)}, bf16[8,2048]{1,0:T(8,128)(2,1)S(1)}, u32[]{:S(2)}, u32[]{:S(2)}) collective-permute-start(bf16[8,2048]{1,0:T(8,128)(2,1)S(1)} %pad_maximum_fusion.1), channel_id=1, source_target_pairs={{4,0},{8,4},{12,8},{16,12},{20,16},{24,20},{28,24},{5,1},{9,5},{13... | collective-permute-start | bytes 98312 | tf_op jit(solution)/shard_map/ppermute | solution.py:491
  34.6 0.0 copy-done.3
  34.6 0.7 copy.20.refs_9_
  35.3 11.2 %pairs.1.refs_10_ = f32[16,1,128]{2,1,0:T(1,128)} custom-call(bf16[2048,1024]{1,0:T(8,128)(2,1)} %get-tuple-element.19.x_ref.refs_11_, bf16[2048,1024]{1,0:T(8,128)(2,1)} %get-tuple-element.20.h_ref.refs_12_, f32[128,16]{1,0:T(8,128)} %copy.19.refs_7_.rate_ref.refs_8_), custom_call_target="tpu_custom_call" | custom-call | flops 4000000000 | bytes 17000000 | tf_op jit(solution)/shard_map/pairs/pallas_call | solution.py:537
  46.5 0.0 collective-permute-done.1.refs_6_
  46.5 0.0 copy-start.2
  46.5 2.1 %all-to-all-done.refs_15_ = f32[8,256,128]{2,1,0:T(8,128)S(1)} async-done(((f32[8,256,128]{2,1,0:T(8,128)}), f32[8,256,128]{2,1,0:T(8,128)S(1)}, u32[]{:S(2)}, u32[]{:S(2)}) %all-to-all-start) | async-done | bytes 1048608 | tf_op jit(solution)/shard_map/all_to_all | solution.py:536
  48.6 0.0 copy-start
  48.6 0.0 copy-done.2
  48.6 1.0 copy-done
  49.6 39.0 %finish.1 = (bf16[1024,2048]{1,0:T(8,128)(2,1)}, bf16[1024,2048]{1,0:T(8,128)(2,1)}, bf16[1024,2048]{1,0:T(8,128)(2,1)}, bf16[1024,2048]{1,0:T(8,128)(2,1)}, bf16[8,16,2048]{2,1,0:T(8,128)(2,1)}) custom-call(s32[1]{0:T(128)} %bitcast.refs_0_, bf16[1024,2048]{1,0:T(8,128)(2,1)} %refs_1_.3, bf16[1024,2048]{1,0:T(8,128)(2,1)} %refs_2_.3, ...), custom_call_target="tpu_custom_call" | custom-call | flops 8000000000 | bytes 50000000 | tf_op jit(solution)/shard_map/finish/pallas_call | solution.py:555
  88.6 13.1 %all_to_all.10 = bf16[8,16,2048]{2,1,0:T(8,128)(2,1)S(1)} all-to-all(bf16[8,16,2048]{2,1,0:T(8,128)(2,1)} %get-tuple-element.31), channel_id=1, replica_groups=mesh['ctx'=8,'tp'=4] {'ctx'}, dimensions={0} | all-to-all | bytes 1048576 | tf_op jit(solution)/shard_map/all_to_all | solution.py:582
  101.7 0.1 convert_reduce_fusion
  101.8 0.1 add.8
  101.9 0.7 copy.21
  102.6 0.7 reshape.23
  (3 shorter events, 0.1 us)
Async XLA Ops:
  2.3 3.8 %collective-permute-start = (bf16[6,2048]{1,0:T(8,128)(2,1)S(1)}, bf16[6,2048]{1,0:T(8,128)(2,1)S(1)}, u32[]{:S(2)}, u32[]{:S(2)}) collective-permute-start(bf16[6,2048]{1,0:T(8,128)(2,1)S(1)} %pad_maximum_fusion), channel_id=1, source_target_pairs={{0,4},{4,8},{8,12},{12,16},{16,20},{20,24},{24,28},{1,5},{5,9},{9,... | collective-permute-start | bytes 73736 | tf_op jit(solution)/shard_map/ppermute | solution.py:487
  6.2 0.6 copy-start.1
  6.8 26.4 %slice-start = ((bf16[1024,2048]{1,0:T(8,128)(2,1)}), bf16[2,2048]{1,0:T(2,128)(2,1)S(1)}, s32[]{:S(2)}) async-start(bf16[1024,2048]{1,0:T(8,128)(2,1)} %refs_4_.3), calls=%async_computation.2 | async-start | bytes 16384 | tf_op jit(solution)/shard_map/slice | solution.py:492
  6.8 27.8 %copy-start.3 = (f32[128,16]{0,1:T(8,128)S(1)}, f32[128,16]{0,1:T(8,128)}, u32[]{:S(2)}) copy-start(f32[128,16]{0,1:T(8,128)} %param.12) | copy-start | bytes 24580
  26.6 22.0 %all-to-all-start = ((f32[8,256,128]{2,1,0:T(8,128)}), f32[8,256,128]{2,1,0:T(8,128)S(1)}, u32[]{:S(2)}, u32[]{:S(2)}) async-start(f32[8,256,128]{2,1,0:T(8,128)} %get-tuple-element.23), calls=%async_computation | async-start | bytes 2097152 | tf_op jit(solution)/shard_map/all_to_all | solution.py:536
  33.3 13.2 %collective-permute-start.1 = (bf16[8,2048]{1,0:T(8,128)(2,1)S(1)}, bf16[8,2048]{1,0:T(8,128)(2,1)S(1)}, u32[]{:S(2)}, u32[]{:S(2)}) collective-permute-start(bf16[8,2048]{1,0:T(8,128)(2,1)S(1)} %pad_maximum_fusion.1), channel_id=1, source_target_pairs={{4,0},{8,4},{12,8},{16,12},{20,16},{24,20},{28,24},{5,1},{9,5},{13... | collective-permute-start | bytes 98312 | tf_op jit(solution)/shard_map/ppermute | solution.py:491
  46.5 2.1 %copy-start.2 = (bf16[8,2048]{1,0:T(8,128)(2,1)}, bf16[8,2048]{1,0:T(8,128)(2,1)S(1)}, u32[]{:S(2)}) copy-start(bf16[8,2048]{1,0:T(8,128)(2,1)S(1)} %collective-permute-done.1.refs_6_) | copy-start | bytes 98308
  48.6 1.0 copy-start
